TPU v7x, 32 devices: a whole 2x2x4 slice. The times are simulated.
32 devices in a mesh: section: 2 (over core), dp: 4 (over z), tensor: 4 (over y, x).
Axes of the slice: x: 2, y: 2, z: 4, core: 2. Of those that a mesh axis runs over, the one named last changes fastest.
Arguments:
- tokens: bfloat16 [32, 160, 768], P(('dp', 'tensor')), may hold values from -1.7265625 to 1.7265625
- cotangent: bfloat16 [32, 160, 768], P(('dp', 'tensor')), may hold values from -6 to 6
- lengths: int32 [32], P('dp'), may hold values from 80 to 160, as said below
- chain_type: int32 [32], P('dp'), may hold values 0 or 1
- qkv_weight: bfloat16 [2, 2, 768, 3, 768], P('section', None, None, None, 'tensor'), may hold values from -0.21875 to 0.21875
- qkv_bias: float32 [2, 2, 2, 768], P('section', None, None, 'tensor'), may hold values from -0.8 to 0.8
- out_weight: bfloat16 [2, 2, 768, 768], P('section', None, 'tensor'), may hold values from -0.625 to 0.625
- out_bias: float32 [2, 2, 768], P('section'), may hold values from -0.8 to 0.8
- ffn_in: bfloat16 [2, 2, 768, 3072], P('section', None, None, 'tensor'), may hold values from -0.21875 to 0.21875
- ffn_in_bias: float32 [2, 2, 3072], P('section', None, 'tensor'), may hold values from -0.8 to 0.8
- ffn_out: bfloat16 [2, 2, 3072, 768], P('section', None, 'tensor'), may hold values from -0.109375 to 0.109375
- ffn_out_bias: float32 [2, 2, 768], P('section'), may hold values from -0.8 to 0.8
- norm_gain: float32 [2, 2, 2, 768], P('section'), may hold values from 0.5 to 1.5
- norm_bias: float32 [2, 2, 2, 768], P('section'), may hold values from -0.8 to 0.8
Outputs:
- acts: bfloat16 [2, 32, 160, 768], P('section', ('dp', 'tensor'))
- in_grad: float32 [2, 32, 160, 768], P('section', ('dp', 'tensor'))
- qkv_weight_grad: float32 [2, 2, 768, 3, 768], P('section', None, 'dp', None, 'tensor')
- qkv_bias_grad: float32 [2, 2, 2, 768], P('section', None, None, 'tensor')
- out_weight_grad: float32 [2, 2, 768, 768], P('section', None, 'tensor', 'dp')
- out_bias_grad: float32 [2, 2, 768], P('section')
- ffn_in_grad: float32 [2, 2, 768, 3072], P('section', None, 'dp', 'tensor')
- ffn_in_bias_grad: float32 [2, 2, 3072], P('section', None, 'tensor')
- ffn_out_grad: float32 [2, 2, 3072, 768], P('section', None, 'tensor', 'dp')
- ffn_out_bias_grad: float32 [2, 2, 768], P('section')
- norm_gain_grad: float32 [2, 2, 2, 768], P('section')
- norm_bias_grad: float32 [2, 2, 2, 768], P('section')
Inputs may be any that keep to these rules, and one draw needn't show every extreme that they name: `lengths`: real tokens of a chain; the other positions of its 160 are padding. `chain_type`: 0 for a heavy chain, 1 for a light chain.
All inputs are finite; a program needn't handle non-finite values. No bound on the sum of `chain_type` on one device may be relied on, other than what follows from the above.
Results may differ from a plain program's by a relative error of at most 0.02.
Values may be sent and summed in bfloat16 or wider, within the bound.
No kernel may reach another device: no remote copies, remote signals or barrier semaphores. Data moves between devices by JAX's collectives and lax.ppermute only.
A program may use at most 192 MiB of HBM per device.

v0:
```python
import math

import jax
import jax.numpy as jnp
from jax import lax
from jax.sharding import PartitionSpec as P

HEAD_DIM = 64
TYPES = 2
MICRO = 2


HIGH = lax.Precision.HIGHEST
norm_eps = 1e-06
half_root = 0.7071067811865476
density = 0.3989422804014327


def shifted(value, axis, steps):
    count = lax.axis_size(axis)
    leading, last = (max(0, -steps), min(count, count - steps))
    return lax.ppermute(value, axis, [(source, source + steps) for source in range(leading, last)])


def pick(onehot, table):
    return jnp.einsum("ct,t...->c...", onehot, table, precision=HIGH)


def by_type(onehot, chain_terms):
    return jnp.einsum("ct,c...->t...", onehot, chain_terms, precision=HIGH)


def type_rows(tags):
    return (tags[:, None] == jnp.arange(TYPES)[None, :]).astype(jnp.float32)


def row_mask(onehot, type_index, rows):
    shape = (-1,) + (1,) * (rows.ndim - 1)
    return rows * onehot[:, type_index].astype(rows.dtype).reshape(shape)


def apply_typed(onehot, rows, spec, table):
    running = None
    for type_index in range(TYPES):
        term = jnp.einsum(
            spec,
            row_mask(onehot, type_index, rows),
            table[type_index],
            preferred_element_type=jnp.float32,
        )
        running = term if running is None else running + term
    return running


def grad_typed(onehot, left, right, spec):
    return jnp.stack(
        [
            jnp.einsum(
                spec, row_mask(onehot, type_index, left), right, preferred_element_type=jnp.float32
            )
            for type_index in range(TYPES)
        ]
    )


def layer_norm(values, gain, shift):
    center = values - jnp.mean(values, axis=-1, keepdims=True)
    inv_dev = lax.rsqrt(jnp.mean(center * center, axis=-1, keepdims=True) + norm_eps)
    normal = center * inv_dev
    return (normal * gain + shift, (normal, inv_dev))


def norm_back(grad_in, normal, inv_dev, gain):
    scaled = grad_in * gain
    return inv_dev * (
        scaled
        - jnp.mean(scaled, axis=-1, keepdims=True)
        - normal * jnp.mean(scaled * normal, axis=-1, keepdims=True)
    )


def masked_scores(query_rows, key_rows, key_keep):
    scores = jnp.einsum(
        "cqhe,ckhe->chqk", query_rows, key_rows, preferred_element_type=jnp.float32
    ) * (1.0 / math.sqrt(HEAD_DIM))
    return jnp.where(key_keep[:, None, None, :], scores, -1000000000.0)


def forward(own_rows, tags_all, tags_own, lens_all, params):
    qkv_w, qkv_b, out_w, out_b, in_w, in_b, back_w, back_b, gains, shifts = params
    onehot_all = type_rows(tags_all)
    onehot_own = type_rows(tags_own)
    full_rows = lax.all_gather(own_rows, "tensor", axis=0, tiled=True)
    chains, length, full_width = full_rows.shape
    proj = apply_typed(onehot_all, full_rows, "cld,dke->clke", qkv_w)
    bias_rows = pick(onehot_all, qkv_b)
    local_width = proj.shape[-1]
    heads_shape = (chains, length, local_width // HEAD_DIM, HEAD_DIM)
    query_rows = (proj[:, :, 0] + bias_rows[:, None, 0]).astype(jnp.bfloat16).reshape(heads_shape)
    key_rows = proj[:, :, 1].astype(jnp.bfloat16).reshape(heads_shape)
    value_rows = (proj[:, :, 2] + bias_rows[:, None, 1]).astype(jnp.bfloat16).reshape(heads_shape)
    key_keep = jnp.arange(length)[None, :] < lens_all[:, None]
    scores = masked_scores(query_rows, key_rows, key_keep)
    row_peak = jnp.max(scores, axis=-1, keepdims=True)
    exp_scores = jnp.exp(scores - row_peak)
    row_total = jnp.sum(exp_scores, axis=-1, keepdims=True)
    attn_probs = (exp_scores / row_total).astype(jnp.bfloat16)
    log_total = row_peak + jnp.log(row_total)
    attended = jnp.einsum(
        "chqk,ckhe->cqhe", attn_probs, value_rows, preferred_element_type=jnp.float32
    )
    attended = attended.reshape(chains, length, local_width).astype(jnp.bfloat16)
    row_piece = attended
    sel_piece = onehot_all
    attn_sum = lax.psum_scatter(
        apply_typed(sel_piece, row_piece, "cle,ed->cld", out_w).astype(jnp.bfloat16),
        "tensor",
        scatter_dimension=0,
        tiled=True,
    ).astype(jnp.float32)
    gain_own = pick(onehot_own, gains)
    shift_own = pick(onehot_own, shifts)
    mixed = own_rows.astype(jnp.float32) + attn_sum + pick(onehot_own, out_b)[:, None]
    normed, first_stat = layer_norm(mixed, gain_own[:, None, 0], shift_own[:, None, 0])
    normed_full = lax.all_gather(normed.astype(jnp.bfloat16), "tensor", axis=0, tiled=True)
    pre_act = (
        apply_typed(onehot_all, normed_full, "cld,df->clf", in_w) + pick(onehot_all, in_b)[:, None]
    )
    hidden = (0.5 * pre_act * (1.0 + lax.erf(pre_act * half_root))).astype(jnp.bfloat16)
    row_piece = hidden
    sel_piece = onehot_all
    ffn_sum = lax.psum_scatter(
        apply_typed(sel_piece, row_piece, "clf,fd->cld", back_w).astype(jnp.bfloat16),
        "tensor",
        scatter_dimension=0,
        tiled=True,
    ).astype(jnp.float32)
    summed = normed + ffn_sum + pick(onehot_own, back_b)[:, None]
    output, second_stat = layer_norm(summed, gain_own[:, None, 1], shift_own[:, None, 1])
    saved = (
        full_rows,
        query_rows,
        key_rows,
        value_rows,
        key_keep,
        log_total,
        attended,
        normed_full,
        pre_act,
        hidden,
        first_stat,
        second_stat,
    )
    return (output, saved)


def backward(grad_out, saved, tags_all, tags_own, params):
    (
        full_rows,
        query_rows,
        key_rows,
        value_rows,
        key_keep,
        log_total,
        attended,
        normed_full,
        pre_act,
        hidden,
        first_stat,
        second_stat,
    ) = saved
    qkv_w, qkv_b, out_w, out_b, in_w, in_b, back_w, back_b, gains, shifts = params
    onehot_all = type_rows(tags_all)
    onehot_own = type_rows(tags_own)
    gain_own = pick(onehot_own, gains)
    second_grad = norm_back(grad_out, second_stat[0], second_stat[1], gain_own[:, None, 1])
    gain_two = jnp.sum(grad_out * second_stat[0], axis=1)
    shift_two = jnp.sum(grad_out, axis=1)
    ffn_full = lax.all_gather(second_grad.astype(jnp.bfloat16), "tensor", axis=0, tiled=True)
    hidden_grad = apply_typed(onehot_all, ffn_full, "cld,fd->clf", back_w)
    back_terms = grad_typed(onehot_all, hidden, ffn_full, "clf,cld->fd")
    gelu_slope = 0.5 * (1.0 + lax.erf(pre_act * half_root)) + pre_act * density * jnp.exp(
        -0.5 * pre_act * pre_act
    )
    pre_grad = (hidden_grad * gelu_slope).astype(jnp.bfloat16)
    in_terms = grad_typed(onehot_all, normed_full, pre_grad, "cld,clf->df")
    in_bias_terms = jnp.sum(pre_grad.astype(jnp.float32), axis=1)
    row_piece = pre_grad
    sel_piece = onehot_all
    normed_grad = (
        lax.psum_scatter(
            apply_typed(sel_piece, row_piece, "clf,df->cld", in_w).astype(jnp.bfloat16),
            "tensor",
            scatter_dimension=0,
            tiled=True,
        ).astype(jnp.float32)
        + second_grad
    )
    first_grad = norm_back(normed_grad, first_stat[0], first_stat[1], gain_own[:, None, 0])
    gain_one = jnp.sum(normed_grad * first_stat[0], axis=1)
    shift_one = jnp.sum(normed_grad, axis=1)
    attn_full = lax.all_gather(first_grad.astype(jnp.bfloat16), "tensor", axis=0, tiled=True)
    out_terms = grad_typed(onehot_all, attended, attn_full, "cle,cld->ed")
    attended_grad = apply_typed(onehot_all, attn_full, "cld,ed->cle", out_w)
    attended_grad = attended_grad.astype(jnp.bfloat16).reshape(query_rows.shape)
    scores = masked_scores(query_rows, key_rows, key_keep)
    attn_probs = jnp.exp(scores - log_total)
    value_grad = jnp.einsum(
        "chqk,cqhe->ckhe",
        attn_probs.astype(jnp.bfloat16),
        attended_grad,
        preferred_element_type=jnp.float32,
    )
    probs_grad = jnp.einsum(
        "cqhe,ckhe->chqk", attended_grad, value_rows, preferred_element_type=jnp.float32
    )
    score_grad = (
        attn_probs * (probs_grad - jnp.sum(attn_probs * probs_grad, axis=-1, keepdims=True))
    ).astype(jnp.bfloat16)
    factor = 1.0 / math.sqrt(HEAD_DIM)
    query_grad = (
        jnp.einsum("chqk,ckhe->cqhe", score_grad, key_rows, preferred_element_type=jnp.float32)
        * factor
    )
    key_grad = (
        jnp.einsum("chqk,cqhe->ckhe", score_grad, query_rows, preferred_element_type=jnp.float32)
        * factor
    )
    chains, length = (query_rows.shape[0], query_rows.shape[1])
    proj_grad = (
        jnp.stack([query_grad, key_grad, value_grad], axis=2)
        .reshape(chains, length, 3, -1)
        .astype(jnp.bfloat16)
    )
    qkv_terms = grad_typed(onehot_all, full_rows, proj_grad, "cld,clke->dke")
    proj_sums = jnp.sum(proj_grad.astype(jnp.float32), axis=1)
    bias_terms = jnp.stack([proj_sums[:, 0], proj_sums[:, 2]], axis=1)
    row_piece = proj_grad
    sel_piece = onehot_all
    input_grad = (
        lax.psum_scatter(
            apply_typed(sel_piece, row_piece, "clke,dke->cld", qkv_w).astype(jnp.bfloat16),
            "tensor",
            scatter_dimension=0,
            tiled=True,
        ).astype(jnp.float32)
        + first_grad
    )
    large = (qkv_terms, out_terms, in_terms, back_terms)
    tensor_small = (by_type(onehot_all, bias_terms), by_type(onehot_all, in_bias_terms))
    shard_small = (
        by_type(onehot_own, jnp.sum(first_grad, axis=1)),
        by_type(onehot_own, jnp.sum(second_grad, axis=1)),
        by_type(onehot_own, jnp.stack([gain_one, gain_two], axis=1)),
        by_type(onehot_own, jnp.stack([shift_one, shift_two], axis=1)),
    )
    return (input_grad, large, tensor_small, shard_small)


def accumulate(running, addend):
    if running is None:
        return addend
    return jax.tree.map(jnp.add, running, addend)


def body(
    tokens,
    cotangent,
    lengths,
    chain_type,
    qkv_weight,
    qkv_bias,
    out_weight,
    out_bias,
    ffn_in,
    ffn_in_bias,
    ffn_out,
    ffn_out_bias,
    norm_gain,
    norm_bias,
):
    section_rank = lax.axis_index("section")
    tensor_rank = lax.axis_index("tensor")
    tensor_count = lax.axis_size("tensor")
    per_batch = tokens.shape[0] // MICRO
    params = tuple(
        (
            weight[0]
            for weight in (
                qkv_weight,
                qkv_bias,
                out_weight,
                out_bias,
                ffn_in,
                ffn_in_bias,
                ffn_out,
                ffn_out_bias,
                norm_gain,
                norm_bias,
            )
        )
    )
    tag_grid = chain_type.reshape(tensor_count, MICRO, per_batch)
    len_grid = lengths.reshape(tensor_count, MICRO, per_batch)
    first_section = section_rank == 0
    last_section = section_rank == 1

    def batch_ints(batch_index):
        tags_all = jnp.take(tag_grid, batch_index, axis=1).reshape(-1)
        lens_all = jnp.take(len_grid, batch_index, axis=1).reshape(-1)
        tags_own = lax.dynamic_slice_in_dim(tags_all, tensor_rank * per_batch, per_batch, 0)
        return (tags_all, tags_own, lens_all)

    row_shape = (per_batch,) + tokens.shape[1:]
    received = jnp.zeros(row_shape, jnp.bfloat16)
    section_inputs = []
    section_outputs = []
    section_saves = []
    for step_index in range(MICRO + 1):
        batch_index = jnp.where(
            first_section, min(step_index, MICRO - 1), max(step_index - 1, 0)
        ).astype(jnp.int32)
        source = min(step_index, MICRO - 1) * per_batch
        layer_in = jnp.where(first_section, tokens[source : source + per_batch], received)
        tags_all, tags_own, lens_all = batch_ints(batch_index)
        output, saved = forward(layer_in, tags_all, tags_own, lens_all, params)
        output_low = output.astype(jnp.bfloat16)
        if step_index < MICRO:
            received = shifted(output_low, "section", 1)
        section_inputs.append(layer_in)
        section_outputs.append(output_low)
        section_saves.append(saved)
    acts = jnp.concatenate(
        [
            jnp.where(first_section, section_outputs[index_mb], section_outputs[index_mb + 1])
            for index_mb in range(MICRO)
        ],
        axis=0,
    )
    grad_received = jnp.zeros(row_shape, jnp.bfloat16)
    input_grads = []
    large_total = None
    tensor_total = None
    shard_total = None
    for step_index in range(MICRO + 1):
        batch_index = jnp.where(
            last_section, min(step_index, MICRO - 1), max(step_index - 1, 0)
        ).astype(jnp.int32)
        valid = jnp.where(last_section, step_index < MICRO, step_index >= 1)
        source = min(step_index, MICRO - 1) * per_batch
        grad_in = jnp.where(
            last_section,
            cotangent[source : source + per_batch].astype(jnp.float32),
            grad_received.astype(jnp.float32),
        )
        grad_in = jnp.where(valid, grad_in, 0.0)
        upper = min(step_index + 1, MICRO)
        lower = max(step_index - 1, 0)
        tags_all, tags_own, lens_all = batch_ints(batch_index)
        layer_in = jnp.where(last_section, section_inputs[upper], section_inputs[lower])
        unused, saved = forward(layer_in, tags_all, tags_own, lens_all, params)
        input_grad, large, tensor_small, shard_small = backward(
            grad_in, saved, tags_all, tags_own, params
        )
        if step_index < MICRO:
            grad_received = shifted(input_grad.astype(jnp.bfloat16), "section", -1)
        input_grads.append(input_grad)
        large_total = accumulate(large_total, large)
        tensor_total = accumulate(tensor_total, tensor_small)
        shard_total = accumulate(shard_total, shard_small)
    large_total = (
        lax.psum_scatter(
            large_total[0].astype(jnp.bfloat16), "dp", scatter_dimension=1, tiled=True
        ).astype(jnp.float32),
        lax.psum_scatter(
            large_total[1].astype(jnp.bfloat16), "dp", scatter_dimension=2, tiled=True
        ).astype(jnp.float32),
        lax.psum_scatter(
            large_total[2].astype(jnp.bfloat16), "dp", scatter_dimension=1, tiled=True
        ).astype(jnp.float32),
        lax.psum_scatter(
            large_total[3].astype(jnp.bfloat16), "dp", scatter_dimension=2, tiled=True
        ).astype(jnp.float32),
    )
    tensor_sums = lax.psum(tensor_total, "dp")
    shard_sums = lax.psum(shard_total, ("dp", "tensor"))
    in_grad = jnp.concatenate(
        [
            jnp.where(last_section, input_grads[index_mb], input_grads[index_mb + 1])
            for index_mb in range(MICRO)
        ],
        axis=0,
    )
    return (
        acts[None],
        in_grad[None],
        large_total[0][None],
        tensor_sums[0][None],
        large_total[1][None],
        shard_sums[0][None],
        large_total[2][None],
        tensor_sums[1][None],
        large_total[3][None],
        shard_sums[1][None],
        shard_sums[2][None],
        shard_sums[3][None],
    )


def solution(mesh):
    placed = (
        P(("dp", "tensor"), None, None),
        P(("dp", "tensor"), None, None),
        P("dp"),
        P("dp"),
        P("section", None, None, None, "tensor"),
        P("section", None, None, "tensor"),
        P("section", None, "tensor", None),
        P("section", None, None),
        P("section", None, None, "tensor"),
        P("section", None, "tensor"),
        P("section", None, "tensor", None),
        P("section", None, None),
        P("section", None, None, None),
        P("section", None, None, None),
    )
    return jax.shard_map(
        body,
        mesh=mesh,
        in_specs=placed,
        out_specs=(
            P("section", ("dp", "tensor"), None, None),
            P("section", ("dp", "tensor"), None, None),
            P("section", None, "dp", None, "tensor"),
            P("section", None, None, "tensor"),
            P("section", None, "tensor", "dp"),
            P("section", None, None),
            P("section", None, "dp", "tensor"),
            P("section", None, "tensor"),
            P("section", None, "tensor", "dp"),
            P("section", None, None),
            P("section", None, None, None),
            P("section", None, None, None),
        ),
        check_vma=False,
    )
```

profile of v0, /device:TPU:0, one launch (start us, length us, event | category | flops | bytes accessed | tf_op | source)
XLA Modules:
  0.0 1010.8 jit_solution(2207088833718320604)
XLA Ops:
  10.6 14.4 %all_gather.54 = bf16[4,160,768]{2,1,0:T(8,128)(2,1)S(1)} all-gather(bf16[1,160,768]{2,1,0:T(8,128)(2,1)S(1)} %slice_select_fusion), channel_id=1, replica_groups=mesh['section'=2,'dp'=4,'tensor'=4] {'tensor'}, dimensions={0}, use_global_device_ids=true | all-gather | bytes 1228800 | tf_op jit(solution)/shard_map/all_gather | solution.py:93
  54.7 15.4 %reduce-scatter.68.cloned.1.call-done = bf16[1,160,768]{2,1,0:T(8,128)(2,1)} async-done(((bf16[4,160,768]{2,1,0:T(8,128)(2,1)}), bf16[1,160,768]{2,1,0:T(8,128)(2,1)}) %reduce-scatter.68.cloned.1.call-update) | async-done | bytes 245776
  73.6 12.9 %all_gather.55 = bf16[4,160,768]{2,1,0:T(8,128)(2,1)S(1)} all-gather(bf16[1,160,768]{2,1,0:T(8,128)(2,1)S(1)} %fusion.356), channel_id=1, replica_groups=mesh['section'=2,'dp'=4,'tensor'=4] {'tensor'}, dimensions={0}, use_global_device_ids=true | all-gather | bytes 1228800 | tf_op jit(solution)/shard_map/all_gather | solution.py:125
  94.1 25.6 %reduce-scatter.70.cloned.1.call-done = bf16[1,160,768]{2,1,0:T(8,128)(2,1)} async-done(((bf16[4,160,768]{2,1,0:T(8,128)(2,1)}), bf16[1,160,768]{2,1,0:T(8,128)(2,1)}) %reduce-scatter.70.cloned.1.call-update) | async-done | bytes 245776
  128.8 12.4 %all_gather.56 = bf16[4,160,768]{2,1,0:T(8,128)(2,1)S(1)} all-gather(bf16[1,160,768]{2,1,0:T(8,128)(2,1)S(1)} %get-tuple-element.167), channel_id=1, replica_groups=mesh['section'=2,'dp'=4,'tensor'=4] {'tensor'}, dimensions={0}, use_global_device_ids=true | all-gather | bytes 1228800 | tf_op jit(solution)/shard_map/all_gather | solution.py:93
  157.6 16.3 %all_gather.60 = bf16[4,160,768]{2,1,0:T(8,128)(2,1)S(1)} all-gather(bf16[1,160,768]{2,1,0:T(8,128)(2,1)S(1)} %get-tuple-element.166), channel_id=1, replica_groups=mesh['section'=2,'dp'=4,'tensor'=4] {'tensor'}, dimensions={0}, use_global_device_ids=true | all-gather | bytes 1228800 | tf_op jit(solution)/shard_map/all_gather | solution.py:93
  195.6 15.4 %all_gather.57 = bf16[4,160,768]{2,1,0:T(8,128)(2,1)S(1)} all-gather(bf16[1,160,768]{2,1,0:T(8,128)(2,1)S(1)} %fusion.357), channel_id=1, replica_groups=mesh['section'=2,'dp'=4,'tensor'=4] {'tensor'}, dimensions={0}, use_global_device_ids=true | all-gather | bytes 1228800 | tf_op jit(solution)/shard_map/all_gather | solution.py:125
  216.7 4.5 reduce-scatter.80.cloned.1.call-done
  224.7 18.1 %all_gather.61 = bf16[4,160,768]{2,1,0:T(8,128)(2,1)S(1)} all-gather(bf16[1,160,768]{2,1,0:T(8,128)(2,1)S(1)} %fusion.327), channel_id=1, replica_groups=mesh['section'=2,'dp'=4,'tensor'=4] {'tensor'}, dimensions={0}, use_global_device_ids=true | all-gather | bytes 1228800 | tf_op jit(solution)/shard_map/all_gather | solution.py:125
  259.8 25.7 %reduce-scatter.82.cloned.1.call-done = bf16[1,160,768]{2,1,0:T(8,128)(2,1)} async-done(((bf16[4,160,768]{2,1,0:T(8,128)(2,1)}), bf16[1,160,768]{2,1,0:T(8,128)(2,1)}) %reduce-scatter.82.cloned.1.call-update) | async-done | bytes 245776
  290.1 12.8 %all_gather.62 = bf16[4,160,768]{2,1,0:T(8,128)(2,1)S(1)} all-gather(bf16[1,160,768]{2,1,0:T(8,128)(2,1)S(1)} %get-tuple-element.162), channel_id=1, replica_groups=mesh['section'=2,'dp'=4,'tensor'=4] {'tensor'}, dimensions={0}, use_global_device_ids=true | all-gather | bytes 1228800 | tf_op jit(solution)/shard_map/all_gather | solution.py:179
  311.6 16.9 %all_gather.64 = bf16[4,160,768]{2,1,0:T(8,128)(2,1)S(1)} all-gather(bf16[1,160,768]{2,1,0:T(8,128)(2,1)S(1)} %get-tuple-element.160), channel_id=1, replica_groups=mesh['section'=2,'dp'=4,'tensor'=4] {'tensor'}, dimensions={0}, use_global_device_ids=true | all-gather | bytes 1228800 | tf_op jit(solution)/shard_map/all_gather | solution.py:93
  332.5 14.7 %all_gather.68 = bf16[4,160,768]{2,1,0:T(8,128)(2,1)S(1)} all-gather(bf16[1,160,768]{2,1,0:T(8,128)(2,1)S(1)} %broadcast_select_fusion), channel_id=1, replica_groups=mesh['section'=2,'dp'=4,'tensor'=4] {'tensor'}, dimensions={0}, use_global_device_ids=true | all-gather | bytes 1228800 | tf_op jit(solution)/shard_map/all_gather | solution.py:93
  356.4 12.0 %all_gather.58 = bf16[4,160,768]{2,1,0:T(8,128)(2,1)} all-gather(bf16[1,160,768]{2,1,0:T(8,128)(2,1)S(1)} %copy-done.13), channel_id=1, replica_groups=mesh['section'=2,'dp'=4,'tensor'=4] {'tensor'}, dimensions={0}, use_global_device_ids=true | all-gather | bytes 1228800 | tf_op jit(solution)/shard_map/all_gather | solution.py:93
  431.7 14.7 %all_gather.63 = bf16[4,160,768]{2,1,0:T(8,128)(2,1)S(1)} all-gather(bf16[1,160,768]{2,1,0:T(8,128)(2,1)S(1)} %convert_element_type.704), channel_id=1, replica_groups=mesh['section'=2,'dp'=4,'tensor'=4] {'tensor'}, dimensions={0}, use_global_device_ids=true | all-gather | bytes 1228800 | tf_op jit(solution)/shard_map/all_gather | solution.py:202
  476.0 11.6 %all_gather.65 = bf16[4,160,768]{2,1,0:T(8,128)(2,1)S(1)} all-gather(bf16[1,160,768]{2,1,0:T(8,128)(2,1)S(1)} %fusion.328), channel_id=1, replica_groups=mesh['section'=2,'dp'=4,'tensor'=4] {'tensor'}, dimensions={0}, use_global_device_ids=true | all-gather | bytes 1228800 | tf_op jit(solution)/shard_map/all_gather | solution.py:125
  512.6 27.2 %reduce-scatter.90.cloned.1.call-done = bf16[1,160,768]{2,1,0:T(8,128)(2,1)} async-done(((bf16[4,160,768]{2,1,0:T(8,128)(2,1)}), bf16[1,160,768]{2,1,0:T(8,128)(2,1)}) %reduce-scatter.90.cloned.1.call-update) | async-done | bytes 245776
  545.5 12.9 %all_gather.66 = bf16[4,160,768]{2,1,0:T(8,128)(2,1)S(1)} all-gather(bf16[1,160,768]{2,1,0:T(8,128)(2,1)S(1)} %get-tuple-element.156), channel_id=1, replica_groups=mesh['section'=2,'dp'=4,'tensor'=4] {'tensor'}, dimensions={0}, use_global_device_ids=true | all-gather | bytes 1228800 | tf_op jit(solution)/shard_map/all_gather | solution.py:179
  568.3 16.7 %all_gather.69 = bf16[4,160,768]{2,1,0:T(8,128)(2,1)S(1)} all-gather(bf16[1,160,768]{2,1,0:T(8,128)(2,1)S(1)} %fusion.329), channel_id=1, replica_groups=mesh['section'=2,'dp'=4,'tensor'=4] {'tensor'}, dimensions={0}, use_global_device_ids=true | all-gather | bytes 1228800 | tf_op jit(solution)/shard_map/all_gather | solution.py:125
  600.6 18.2 %all_gather.67 = bf16[4,160,768]{2,1,0:T(8,128)(2,1)S(1)} all-gather(bf16[1,160,768]{2,1,0:T(8,128)(2,1)S(1)} %convert_element_type.732), channel_id=1, replica_groups=mesh['section'=2,'dp'=4,'tensor'=4] {'tensor'}, dimensions={0}, use_global_device_ids=true | all-gather | bytes 1228800 | tf_op jit(solution)/shard_map/all_gather | solution.py:202
  643.5 4.3 convolution_bitcast_fusion.4
  661.1 9.7 reduce-scatter.94.cloned.1.call-done
  678.3 13.7 %all_gather.70 = bf16[4,160,768]{2,1,0:T(8,128)(2,1)S(1)} all-gather(bf16[1,160,768]{2,1,0:T(8,128)(2,1)S(1)} %get-tuple-element.152), channel_id=1, replica_groups=mesh['section'=2,'dp'=4,'tensor'=4] {'tensor'}, dimensions={0}, use_global_device_ids=true | all-gather | bytes 1228800 | tf_op jit(solution)/shard_map/all_gather | solution.py:179
  711.9 6.9 copy.251
  718.8 8.2 reduce-scatter.100.cloned.1.call-done
  732.1 13.4 %all_gather.71 = bf16[4,160,768]{2,1,0:T(8,128)(2,1)S(1)} all-gather(bf16[1,160,768]{2,1,0:T(8,128)(2,1)S(1)} %convert_element_type.756), channel_id=1, replica_groups=mesh['section'=2,'dp'=4,'tensor'=4] {'tensor'}, dimensions={0}, use_global_device_ids=true | all-gather | bytes 1228800 | tf_op jit(solution)/shard_map/all_gather | solution.py:202
  752.6 11.7 %all_gather.59 = bf16[4,160,768]{2,1,0:T(8,128)(2,1)S(1)} all-gather(bf16[1,160,768]{2,1,0:T(8,128)(2,1)} %get-tuple-element.204), channel_id=1, replica_groups=mesh['section'=2,'dp'=4,'tensor'=4] {'tensor'}, dimensions={0}, use_global_device_ids=true | all-gather | bytes 1228800 | tf_op jit(solution)/shard_map/all_gather | solution.py:125
  821.3 4.7 copy.312
  831.5 19.4 %all-reduce.20 = (f32[1,2,2,192]{3,1,2,0:T(2,128)S(1)}, f32[1,2,768]{2,1,0:T(2,128)}) all-reduce(f32[1,2,2,192]{3,1,2,0:T(2,128)S(1)} %fusion.102, f32[1,2,768]{2,1,0:T(2,128)S(1)} %fusion.101), channel_id=1, replica_groups=mesh['section'=2,'dp'=4,'tensor'=4] {'dp'}, use_global_device_ids=true, to_apply=%region_73.77 | all-reduce | flops 2304 | bytes 18432 | tf_op jit(solution)/shard_map/psum | solution.py:385
  851.9 74.5 %all-reduce.19 = (f32[1,2,768]{2,1,0:T(2,128)}, f32[1,2,768]{2,1,0:T(2,128)}, f32[1,2,2,768]{3,2,1,0:T(2,128)}, f32[1,2,2,768]{3,2,1,0:T(2,128)}) all-reduce(f32[1,2,768]{2,1,0:T(2,128)S(1)} %get-tuple-element.216, f32[1,2,768]{2,1,0:T(2,128)S(1)} %get-tuple-element.215, ...), channel_id=1, replica_groups=mesh['section'=2,'dp'=4,'tensor'=4] {'dp','tensor'}, use_global_device_ids=true, to_apply=%region_78.82 | all-reduce | flops 9216 | bytes 73728 | tf_op jit(solution)/shard_map/psum | solution.py:386
  935.9 23.2 %reduce-scatter.62.cloned.1.call-done = bf16[2,192,768]{2,1,0:T(8,128)(2,1)} async-done(((bf16[2,768,768]{2,1,0:T(8,128)(2,1)}), bf16[2,192,768]{2,1,0:T(8,128)(2,1)}) %reduce-scatter.62.cloned.1.call-update) | async-done | bytes 589840 | tf_op jit(solution)/shard_map/reduce_scatter | solution.py:378
  961.2 38.1 %reduce-scatter.64.cloned.1.call-done = bf16[192,1152]{1,0:T(8,128)(2,1)} async-done(((bf16[768,1152]{1,0:T(8,128)(2,1)}), bf16[192,1152]{1,0:T(8,128)(2,1)}) %reduce-scatter.64.cloned.1.call-update) | async-done | bytes 442384
  (1091 shorter events, 445.7 us)
Async XLA Ops:
  7.2 62.8 %reduce-scatter.68.cloned.1.call-start = ((), (), s32[]{:S(2)}) async-start(), calls=%async_computation.25 | async-start | bytes 1228800
  42.3 77.4 %reduce-scatter.70.cloned.1.call-start = ((), (), s32[]{:S(2)}) async-start(), calls=%async_computation.26 | async-start | bytes 1228800
  45.8 73.9 %copy-start.169 = (f32[768]{0:T(1024)}, f32[768]{0:T(1024)S(1)}, u32[]{:S(2)}) copy-start(f32[768]{0:T(1024)S(1)} %convolution_reduce_fusion.6) | copy-start | bytes 9220
  52.3 67.3 %copy-start.131 = (f32[768]{0:T(1024)}, f32[768]{0:T(1024)S(1)}, u32[]{:S(2)}) copy-start(f32[768]{0:T(1024)S(1)} %get-tuple-element.124) | copy-start | bytes 9220
  52.4 68.8 %copy-start.149 = (f32[768]{0:T(1024)}, f32[768]{0:T(1024)S(1)}, u32[]{:S(2)}) copy-start(f32[768]{0:T(1024)S(1)} %get-tuple-element.123) | copy-start | bytes 9220
  53.2 68.0 %copy-start.129 = (f32[768]{0:T(1024)}, f32[768]{0:T(1024)S(1)}, u32[]{:S(2)}) copy-start(f32[768]{0:T(1024)S(1)} %get-tuple-element.121) | copy-start | bytes 9220
  92.2 99.8 %reduce-scatter.72.cloned.1.call-start = ((), (), s32[]{:S(2)}) async-start(), calls=%async_computation.27 | async-start | bytes 1228800
  121.9 6.8 collective-permute-start
  157.5 63.6 %reduce-scatter.80.cloned.1.call-start = ((), (), s32[]{:S(2)}) async-start(), calls=%async_computation.31 | async-start | bytes 1228800
  191.9 62.9 %reduce-scatter.74.cloned.1.call-start = ((), (), s32[]{:S(2)}) async-start(), calls=%async_computation.28 | async-start | bytes 1228800
  216.6 68.9 %reduce-scatter.82.cloned.1.call-start = ((), (), s32[]{:S(2)}) async-start(), calls=%async_computation.32 | async-start | bytes 1228800
  249.4 177.9 %reduce-scatter.84.cloned.1.call-start = ((), (), s32[]{:S(2)}) async-start(), calls=%async_computation.33 | async-start | bytes 1228800
  250.1 78.4 %copy-start.269 = (bf16[4]{0:T(256)(128)(2,1)}, bf16[4]{0:T(256)(128)(2,1)S(1)}, u32[]{:S(2)}) copy-start(bf16[4]{0:T(256)(128)(2,1)S(1)} %get-tuple-element.220) | copy-start | bytes 28
  250.1 79.4 %copy-start.241 = (bf16[4]{0:T(256)(128)(2,1)}, bf16[4]{0:T(256)(128)(2,1)S(1)}, u32[]{:S(2)}) copy-start(bf16[4]{0:T(256)(128)(2,1)S(1)} %get-tuple-element.219) | copy-start | bytes 28
  257.4 53.1 %collective-permute-start.1 = (bf16[1,160,768]{2,1,0:T(8,128)(2,1)S(1)}, bf16[1,160,768]{2,1,0:T(8,128)(2,1)}, u32[]{:S(2)}, u32[]{:S(2)}) collective-permute-start(bf16[1,160,768]{2,1,0:T(8,128)(2,1)S(1)} %get-tuple-element.149), channel_id=1, source_target_pairs={{0,16},{1,17},{2,18},{3,19},{4,20},{5,21},{6,22},{7,23},{8,24},{9,... | collective-permute-start | bytes 737288 | tf_op jit(solution)/shard_map/ppermute | solution.py:22
  310.4 161.9 %reduce-scatter.88.cloned.1.call-start = ((), (), s32[]{:S(2)}) async-start(), calls=%async_computation.35 | async-start | bytes 1228800
  385.9 119.1 %reduce-scatter.96.cloned.1.call-start = ((), (), s32[]{:S(2)}) async-start(), calls=%async_computation.39 | async-start | bytes 1228800
  410.4 96.3 %reduce-scatter.76.cloned.1.call-start = ((), (), s32[]{:S(2)}) async-start(), calls=%async_computation.29 | async-start | bytes 1228800
  427.2 81.9 %reduce-scatter.86.cloned.1.call-start = ((), (), s32[]{:S(2)}) async-start(), calls=%async_computation.34 | async-start | bytes 1228800
  472.3 67.5 %reduce-scatter.90.cloned.1.call-start = ((), (), s32[]{:S(2)}) async-start(), calls=%async_computation.36 | async-start | bytes 1228800
  494.7 101.6 %reduce-scatter.92.cloned.1.call-start = ((), (), s32[]{:S(2)}) async-start(), calls=%async_computation.37 | async-start | bytes 1228800
  510.9 30.4 %collective-permute-start.2 = (bf16[1,160,768]{2,1,0:T(8,128)(2,1)}, bf16[1,160,768]{2,1,0:T(8,128)(2,1)}, u32[]{:S(2)}, u32[]{:S(2)}) collective-permute-start(bf16[1,160,768]{2,1,0:T(8,128)(2,1)} %fusion.349), channel_id=1, source_target_pairs={{16,0},{17,1},{18,2},{19,3},{20,4},{21,5},{22,6},{23,7},{24,8},{25... | collective-permute-start | bytes 737288 | tf_op jit(solution)/shard_map/ppermute | solution.py:22
  565.9 92.7 %reduce-scatter.98.cloned.1.call-start = ((), (), s32[]{:S(2)}) async-start(), calls=%async_computation.40 | async-start | bytes 1228800
  593.2 77.6 %reduce-scatter.94.cloned.1.call-start = ((), (), s32[]{:S(2)}) async-start(), calls=%async_computation.38 | async-start | bytes 1228800
  643.4 83.6 %reduce-scatter.100.cloned.1.call-start = ((), (), s32[]{:S(2)}) async-start(), calls=%async_computation.41 | async-start | bytes 1228800
  673.0 3.4 collective-permute-start.3
  699.6 226.8 %all-reduce.23.cloned.1.call-start = ((), (), s32[]{:S(2)}) async-start(), calls=%async_computation.24 | async-start | bytes 4718592
  718.8 210.2 %reduce-scatter.66.cloned.1.call-start = ((), (), s32[]{:S(2)}) async-start(), calls=%async_computation.23 | async-start | bytes 737280
  769.5 161.6 %reduce-scatter.78.cloned.1.call-start = ((), (), s32[]{:S(2)}) async-start(), calls=%async_computation.30 | async-start | bytes 1228800
  778.1 155.7 %reduce-scatter.102.cloned.1.call-start = ((), (), s32[]{:S(2)}) async-start(), calls=%async_computation.42 | async-start | bytes 1228800
  788.9 170.2 %reduce-scatter.62.cloned.1.call-start = ((), (), s32[]{:S(2)}) async-start(), calls=%async_computation.21 | async-start | bytes 2949120 | tf_op jit(solution)/shard_map/reduce_scatter | solution.py:378
  799.4 199.8 %reduce-scatter.64.cloned.1.call-start = ((), (), s32[]{:S(2)}) async-start(), calls=%async_computation.22 | async-start | bytes 2211840
  (316 other events, 2272.9 us)
Sparse Core Ops, SparseCore 0:
  42.4 27.5 reduce-scatter.67
  92.3 27.3 reduce-scatter.69
  157.6 28.5 reduce-scatter.71
  192.1 29.0 reduce-scatter.79
  224.5 30.2 reduce-scatter.73
  258.2 27.2 reduce-scatter.81
  310.5 32.2 reduce-scatter.83
  386.0 27.3 reduce-scatter.87
  417.0 29.3 reduce-scatter.95
  449.7 28.5 reduce-scatter.75
  481.9 27.1 reduce-scatter.85
  512.5 27.2 reduce-scatter.89
  566.0 30.2 reduce-scatter.91
  599.7 30.5 reduce-scatter.97
  643.5 27.2 reduce-scatter.93
  699.7 27.2 reduce-scatter.99
  729.2 95.6 all-reduce.22
  827.0 21.2 reduce-scatter.65
  851.9 25.8 reduce-scatter.77
  881.2 27.4 reduce-scatter.101
  911.0 48.0 reduce-scatter.61
  961.4 37.8 reduce-scatter.63
where the time goes:
time: 1020 us; the launch traced here: 1010 us
  blocking collectives  353 us (35%)
  matrix products  225 us (22%)
  waiting for transfers between devices  187 us (18%)
  local copies, waits for them, and re-layouts  124 us (12%)
  other arithmetic  93.4 us (9%)
  between operations  19.4 us (2%)
    unnamed x43, waiting for transfers between devices  162 us
    dot_general x72, matrix products, apply_typed(): jnp.einsum(spec, row_mask(onehot, type_index, rows), table[type_index], p...  109 us
    all_gather x6, blocking collectives, forward(): full_rows = lax.all_gather(own_rows, 'tensor', axis=0, tiled=True)  86.7 us
    all_gather x6, blocking collectives, forward(): lax.all_gather(normed.astype(jnp.bfloat16), 'tensor', axis=0, tiled=True)  86.4 us
    psum x1, blocking collectives, body(): shard_sums = lax.psum(shard_total, ('dp', 'tensor'))  74.5 us
    all_gather x3, blocking collectives, backward(): lax.all_gather(first_grad.astype(jnp.bfloat16), 'tensor', axis=0, tiled=T...  46.4 us
    all_gather x3, blocking collectives, backward(): lax.all_gather(second_grad.astype(jnp.bfloat16), 'tensor', axis=0, tiled=...  39.4 us
    dot_general x24, matrix products, grad_typed(): jnp.einsum(spec, row_mask(onehot, type_index, left), right, preferred_ele...  38.9 us
  transfers between devices with their start and end apart: 26, of which 13 were waited for; matrix products, arithmetic and copies ran while one was open for 35% of the time, Pallas kernels for 0%

commit v1 on v0

v1 whole, which is shorter than its diff:
```python
import functools
import math

import jax
import jax.numpy as jnp
from jax import lax
from jax.experimental import pallas as pl
from jax.experimental.pallas import tpu as pltpu
from jax.sharding import PartitionSpec as P

HEAD_DIM = 64
TYPES = 2
LAYERS = 2
SPLIT = 1
EPS = 1e-06
HALF_ROOT = 0.7071067811865476
DENSITY = 0.3989422804014327
SCALE = 1.0 / math.sqrt(HEAD_DIM)
MIB = 1 << 20

F32 = jnp.float32
BF16 = jnp.bfloat16

OUT_B, BACK_B, GAIN1, GAIN2, SHIFT1, SHIFT2, IN_B, QKV_B = range(0, 16, 2)


def dot(a, b):
    return jnp.dot(a, b, preferred_element_type=F32)


def dot_nt(a, b):
    return lax.dot_general(a, b, (((1,), (1,)), ((), ())), preferred_element_type=F32)


def dot_tn(a, b):
    return lax.dot_general(a, b, (((0,), (0,)), ((), ())), preferred_element_type=F32)


def nested(structure, flat):
    leaves, tree = jax.tree.flatten(structure)
    return jax.tree.unflatten(tree, flat)


def run(name, body, meta, ins, outs, flops=0, limit=16):
    flat_in, flat_out = jax.tree.leaves(ins), jax.tree.leaves(outs)

    def kernel(meta_ref, *refs):
        body(meta_ref, nested(ins, refs[: len(flat_in)]), nested(outs, refs[len(flat_in) :]))

    vmem = pl.BlockSpec(memory_space=pltpu.VMEM)
    moved = sum(math.prod(a.shape) * a.dtype.itemsize for a in flat_in + flat_out)
    results = pl.pallas_call(
        kernel,
        name=name,
        in_specs=[pl.BlockSpec(memory_space=pltpu.SMEM)] + [vmem] * len(flat_in),
        out_specs=[vmem] * len(flat_out),
        out_shape=flat_out,
        compiler_params=pltpu.CompilerParams(vmem_limit_bytes=limit * MIB),
        cost_estimate=pl.CostEstimate(flops=int(flops), bytes_accessed=moved, transcendentals=0),
    )(meta, *flat_in)
    return nested(outs, results)


def arr(shape, dtype=BF16):
    return jax.ShapeDtypeStruct(tuple(shape), dtype)


class Ids:
    def __init__(self, meta, dims):
        self.meta, self.dims = meta, dims
        self.section, self.tensor, self.dp = meta[0], meta[1], meta[2]

    def chain(self, slot):
        return (self.tensor ^ slot) * self.dims.per_chip + self.section

    def kind(self, slot):
        return self.meta[3 + self.chain(slot)]

    def length(self, slot):
        return self.meta[3 + self.dims.group + self.chain(slot)]


def on_weights(ids, layer, own, other, go):
    pl.when(ids.section == layer)(lambda: go(*own))
    pl.when(ids.section != layer)(lambda: go(*other))


class Dims:
    pass


def attention_forward(dims, layer, meta, rows, own, other, small):
    r, slots, length, width = dims.r, dims.slots, dims.length, dims.width

    def body(meta_ref, ins, outs):
        rows, own, other, small = ins
        parts, qkv, att = outs
        ids = Ids(meta_ref, dims)

        def go(qkv_w, out_w):
            for k in range(slots):
                kind = ids.kind(k)
                bias = small[pl.ds(QKV_B + kind, 1), : 3 * width]
                for h in range(SPLIT):
                    qkv[k, h * r : (h + 1) * r, :] = (dot(rows[h][k][...], qkv_w[kind]) + bias).astype(BF16)
                keep = lax.broadcasted_iota(jnp.int32, (1, length), 1) < ids.length(k)
                for c in range(0, width, HEAD_DIM):
                    query = qkv[k, :, c : c + HEAD_DIM]
                    key = qkv[k, :, width + c : width + c + HEAD_DIM]
                    value = qkv[k, :, 2 * width + c : 2 * width + c + HEAD_DIM]
                    scores = jnp.where(keep, dot_nt(query, key) * SCALE, -1e9)
                    expd = jnp.exp(scores - jnp.max(scores, axis=-1, keepdims=True))
                    probs = (expd * (1.0 / jnp.sum(expd, axis=-1, keepdims=True))).astype(BF16)
                    att[k, :, c : c + HEAD_DIM] = dot(probs, value).astype(BF16)
                for h in range(SPLIT):
                    parts[h][k][...] = dot(att[k, h * r : (h + 1) * r, :], out_w[kind]).astype(BF16)

        on_weights(ids, layer, own, other, go)

    outs = (
        [[arr((r, dims.d))] * slots for _ in range(SPLIT)],
        arr((slots, length, 3 * width)),
        arr((slots, length, width)),
    )
    flops = 2 * slots * length * dims.d * 4 * width
    return run(f"attn_fwd{layer}", body, meta, (rows, own, other, small), outs, flops)


def attention_backward(dims, layer, meta, grads, qkv, own, other):
    r, slots, length, width = dims.r, dims.slots, dims.length, dims.width

    def body(meta_ref, ins, outs):
        grads, qkv, own, other = ins
        parts, dqkv = outs
        ids = Ids(meta_ref, dims)

        def go(qkv_w, out_w):
            for k in range(slots):
                kind = ids.kind(k)
                keep = lax.broadcasted_iota(jnp.int32, (1, length), 1) < ids.length(k)
                datt = jnp.concatenate(
                    [dot_nt(grads[h][k][...], out_w[kind]).astype(BF16) for h in range(SPLIT)], axis=0
                )
                for c in range(0, width, HEAD_DIM):
                    query = qkv[k, :, c : c + HEAD_DIM]
                    key = qkv[k, :, width + c : width + c + HEAD_DIM]
                    value = qkv[k, :, 2 * width + c : 2 * width + c + HEAD_DIM]
                    da = datt[:, c : c + HEAD_DIM]
                    scores = jnp.where(keep, dot_nt(query, key) * SCALE, -1e9)
                    expd = jnp.exp(scores - jnp.max(scores, axis=-1, keepdims=True))
                    probs = expd * (1.0 / jnp.sum(expd, axis=-1, keepdims=True))
                    dprobs = dot_nt(da, value)
                    dscores = (
                        probs * (dprobs - jnp.sum(probs * dprobs, axis=-1, keepdims=True))
                    ).astype(BF16)
                    dqkv[k, :, c : c + HEAD_DIM] = (dot(dscores, key) * SCALE).astype(BF16)
                    dqkv[k, :, width + c : width + c + HEAD_DIM] = (
                        dot_tn(dscores, query) * SCALE
                    ).astype(BF16)
                    dqkv[k, :, 2 * width + c : 2 * width + c + HEAD_DIM] = dot_tn(
                        probs.astype(BF16), da
                    ).astype(BF16)
                for h in range(SPLIT):
                    parts[h][k][...] = dot_nt(dqkv[k, h * r : (h + 1) * r, :], qkv_w[kind]).astype(BF16)

        on_weights(ids, layer, own, other, go)

    outs = (
        [[arr((r, dims.d))] * slots for _ in range(SPLIT)],
        arr((slots, length, 3 * width)),
    )
    flops = 2 * slots * length * dims.d * 4 * width
    return run(f"attn_bwd{layer}", body, meta, (grads, qkv, own, other), outs, flops)


def typed_sum(ids, left, right, kind, slots):
    chosen = [
        jnp.where(ids.kind(k) == kind, right[k], jnp.zeros_like(right[k])) for k in range(slots)
    ]
    return dot_tn(jnp.concatenate(left, axis=0), jnp.concatenate(chosen, axis=0))


def joined(refs, k):
    return jnp.concatenate([refs[h][k][...] for h in range(SPLIT)], axis=0)


def row_sums(ids, slots, rows, out, cols):
    for kind in range(TYPES):
        total = jnp.zeros((1, cols), F32)
        for k in range(slots):
            here = jnp.sum(rows(k).astype(F32), axis=0, keepdims=True)
            total = total + jnp.where(ids.kind(k) == kind, here, 0.0)
        out[kind : kind + 1, :cols] = total


def attention_weights(dims, layer, meta, rows, dqkv, grads, att):
    slots, width, d = dims.slots, dims.width, dims.d

    def body(meta_ref, ins, outs):
        rows, dqkv, grads, att = ins
        total, bias = outs
        ids = Ids(meta_ref, dims)
        left = [joined(rows, k) for k in range(slots)]
        back = [joined(grads, k) for k in range(slots)]
        for kind in range(TYPES):
            total[kind, :, : 3 * width] = typed_sum(
                ids, left, [dqkv[k] for k in range(slots)], kind, slots
            ).astype(BF16)
            total[kind, :, 3 * width :] = typed_sum(
                ids, back, [att[k] for k in range(slots)], kind, slots
            ).astype(BF16)
        bias[...] = jnp.zeros_like(bias)
        row_sums(ids, slots, lambda k: dqkv[k], bias, 3 * width)

    outs = (arr((TYPES, d, 4 * width)), arr((TYPES, d), F32))
    flops = 2 * 2 * slots * dims.length * d * 4 * width
    return run(f"attn_dw{layer}", body, meta, (rows, dqkv, grads, att), outs, flops, 24)


def ffn_forward(dims, layer, meta, rows, own, other, small):
    r, slots, hidden = dims.r, dims.slots, dims.hidden

    def body(meta_ref, ins, outs):
        rows, own, other, small = ins
        parts, act, slope = outs
        ids = Ids(meta_ref, dims)

        def go(in_w, back_w):
            for k in range(slots):
                kind = ids.kind(k)
                pre = dot(rows[k][...], in_w[kind]) + small[pl.ds(IN_B + kind, 1), :hidden]
                gate = 0.5 * (1.0 + lax.erf(pre * HALF_ROOT))
                act[k] = (pre * gate).astype(BF16)
                slope[k] = (gate + pre * (DENSITY * jnp.exp(-0.5 * pre * pre))).astype(BF16)
                parts[k][...] = dot(act[k], back_w[kind]).astype(BF16)

        on_weights(ids, layer, own, other, go)

    outs = ([arr((r, dims.d))] * slots, arr((slots, r, hidden)), arr((slots, r, hidden)))
    flops = 4 * slots * r * dims.d * hidden
    return run(f"ffn_fwd{layer}", body, meta, (rows, own, other, small), outs, flops)


def ffn_backward(dims, layer, meta, grads, slope, own, other):
    r, slots, hidden = dims.r, dims.slots, dims.hidden

    def body(meta_ref, ins, outs):
        grads, slope, own, other = ins
        parts, dpre = outs
        ids = Ids(meta_ref, dims)

        def go(in_w, back_w):
            for k in range(slots):
                kind = ids.kind(k)
                dact = dot_nt(grads[k][...], back_w[kind])
                dpre[k] = (dact * slope[k].astype(F32)).astype(BF16)
                parts[k][...] = dot_nt(dpre[k], in_w[kind]).astype(BF16)

        on_weights(ids, layer, own, other, go)

    outs = ([arr((r, dims.d))] * slots, arr((slots, r, hidden)))
    flops = 4 * slots * r * dims.d * hidden
    return run(f"ffn_bwd{layer}", body, meta, (grads, slope, own, other), outs, flops)


def ffn_weights(dims, layer, meta, rows, dpre, grads, act):
    slots, hidden, d = dims.slots, dims.hidden, dims.d

    def body(meta_ref, ins, outs):
        rows, dpre, grads, act = ins
        total, bias = outs
        ids = Ids(meta_ref, dims)
        for step, (left, right) in enumerate(((rows, dpre), (grads, act))):
            left_rows = [joined(left, k) for k in range(slots)]
            right_rows = [joined(right, k) for k in range(slots)]
            for kind in range(TYPES):
                total[TYPES * step + kind] = typed_sum(ids, left_rows, right_rows, kind, slots).astype(BF16)
        row_sums(ids, slots, lambda k: joined(dpre, k), bias, hidden)

    outs = (arr((2 * TYPES, d, hidden)), arr((TYPES, hidden), F32))
    flops = 2 * 4 * slots * dims.length * d * hidden
    split = lambda a: [[a[h][k] for k in range(slots)] for h in range(SPLIT)]
    return run(f"ffn_dw{layer}", body, meta, (rows, dpre, grads, act), outs, flops, 24)


def normalized(values):
    center = values - jnp.mean(values, axis=-1, keepdims=True)
    inv = lax.rsqrt(jnp.mean(center * center, axis=-1, keepdims=True) + EPS)
    return center * inv, inv


def summed(parts):
    total = parts[0][...].astype(F32)
    for part in parts[1:]:
        total = total + part[...].astype(F32)
    return total


def norm_back(grad, normal, inv, gain):
    scaled = grad * gain
    return inv * (
        scaled
        - jnp.mean(scaled, axis=-1, keepdims=True)
        - normal * jnp.mean(scaled * normal, axis=-1, keepdims=True)
    )


def sum_rows(out, values):
    for row, value in enumerate(values):
        out[row : row + 1, :] = jnp.sum(value, axis=0, keepdims=True)
    out[len(values) :, :] = jnp.zeros((out.shape[0] - len(values), out.shape[1]), F32)


def first_norm(dims, layer, meta, own_rows, parts, small):
    r, d = dims.r, dims.d

    def body(meta_ref, ins, outs):
        own_rows, parts, small = ins
        low, normal, inv = outs
        kind = Ids(meta_ref, dims).kind(0)
        mixed = own_rows[...].astype(F32) + summed(parts) + small[pl.ds(OUT_B + kind, 1), :]
        xhat, scale = normalized(mixed)
        normal[...] = xhat
        inv[...] = jnp.broadcast_to(scale, inv.shape)
        low[...] = (xhat * small[pl.ds(GAIN1 + kind, 1), :] + small[pl.ds(SHIFT1 + kind, 1), :]).astype(BF16)

    outs = (arr((r, d)), arr((r, d), F32), arr((r, 128), F32))
    return run(f"norm1_{layer}", body, meta, (own_rows, parts, small), outs)


def second_values(kind, normal, parts, small):
    normed = normal[...] * small[pl.ds(GAIN1 + kind, 1), :] + small[pl.ds(SHIFT1 + kind, 1), :]
    xhat, scale = normalized(normed + summed(parts) + small[pl.ds(BACK_B + kind, 1), :])
    output = xhat * small[pl.ds(GAIN2 + kind, 1), :] + small[pl.ds(SHIFT2 + kind, 1), :]
    return xhat, scale, output.astype(BF16)


def second_norm(dims, layer, meta, normal, parts, small):
    r, d = dims.r, dims.d

    def body(meta_ref, ins, outs):
        normal, parts, small = ins
        low, xhat_ref, inv = outs
        kind = Ids(meta_ref, dims).kind(0)
        xhat, scale, low[...] = second_values(kind, normal, parts, small)
        xhat_ref[...] = xhat
        inv[...] = jnp.broadcast_to(scale, inv.shape)

    outs = (arr((r, d)), arr((r, d), F32), arr((r, 128), F32))
    return run(f"norm2_{layer}", body, meta, (normal, parts, small), outs)


def second_back(kind, grad, xhat, scale, small, second_grad, low, sums):
    value = norm_back(grad, xhat, scale, small[pl.ds(GAIN2 + kind, 1), :])
    second_grad[...] = value
    low[...] = value.astype(BF16)
    sum_rows(sums, (grad * xhat, grad, value))


def last_norm(dims, layer, meta, normal, parts, small, cotangent):
    r, d = dims.r, dims.d

    def body(meta_ref, ins, outs):
        normal, parts, small, cotangent = ins
        act, second_grad, low, sums = outs
        kind = Ids(meta_ref, dims).kind(0)
        xhat, scale, act[...] = second_values(kind, normal, parts, small)
        second_back(kind, cotangent[...].astype(F32), xhat, scale, small, second_grad, low, sums)

    outs = (arr((r, d)), arr((r, d), F32), arr((r, d)), arr((8, d), F32))
    return run(f"norm2_{layer}", body, meta, (normal, parts, small, cotangent), outs)


def between_layers(dims, layer, meta, parts, first_grad, xhat, inv, small):
    r, d = dims.r, dims.d

    def body(meta_ref, ins, outs):
        parts, first_grad, xhat, inv, small = ins
        input_grad, second_grad, low, sums = outs
        kind = Ids(meta_ref, dims).kind(0)
        value = summed(parts) + first_grad[...]
        input_grad[...] = value
        grad = value.astype(BF16).astype(F32)
        second_back(kind, grad, xhat[...], inv[:, :1], small, second_grad, low, sums)

    outs = (arr((r, d), F32), arr((r, d), F32), arr((r, d)), arr((8, d), F32))
    return run(f"between{layer}", body, meta, (parts, first_grad, xhat, inv, small), outs)


def first_back(dims, layer, meta, parts, second_grad, xhat, inv, small):
    r, d = dims.r, dims.d

    def body(meta_ref, ins, outs):
        parts, second_grad, xhat, inv, small = ins
        first_grad, low, sums = outs
        kind = Ids(meta_ref, dims).kind(0)
        grad = summed(parts) + second_grad[...]
        value = norm_back(grad, xhat[...], inv[:, :1], small[pl.ds(GAIN1 + kind, 1), :])
        first_grad[...] = value
        low[...] = value.astype(BF16)
        sum_rows(sums, (grad * xhat[...], grad, value))

    outs = (arr((r, d), F32), arr((r, d)), arr((8, d), F32))
    return run(f"norm1_back{layer}", body, meta, (parts, second_grad, xhat, inv, small), outs)


def input_gradient(dims, layer, meta, parts, first_grad):
    def body(meta_ref, ins, outs):
        parts, first_grad = ins
        outs[...] = summed(parts) + first_grad[...]

    return run(f"input_grad{layer}", body, meta, (parts, first_grad), arr((dims.r, dims.d), F32))


def swap(value, axis, bit):
    count = lax.axis_size(axis)
    return lax.ppermute(value, axis, [(source, source ^ bit) for source in range(count)])


def gather(value, slots):
    return [value] + [swap(value, "tensor", k) for k in range(1, slots)]


def scatter(parts):
    return [parts[0]] + [swap(part, "tensor", k) for k, part in enumerate(parts) if k]


class GradSum:
    def __init__(self, dims, layer, meta, value, name):
        self.dims, self.layer, self.meta, self.value, self.name = dims, layer, meta, value, name
        self.rows = value.shape[1] // dims.dp
        self.other = lax.ppermute(value, "section", [(1 - layer, layer)])
        if dims.dp == 4:
            self.halved()
        else:
            whole = (self.value.astype(F32) + self.other.astype(F32)).astype(BF16)
            self.direct = lax.psum_scatter(whole, "dp", scatter_dimension=1, tiled=True)

    def permute(self, value, bit):
        base = self.layer * self.dims.dp
        pairs = [(base + z, base + (z ^ bit)) for z in range(self.dims.dp)]
        return lax.ppermute(value, ("section", "dp"), pairs)

    def halved(self):
        dims, rows = self.dims, self.rows
        count, _, cols = self.value.shape

        def part(ref, chunk):
            return ref[:, pl.ds(pl.multiple_of(chunk * rows, 16), rows), :].astype(F32)

        def first(meta_ref, ins, outs):
            value, other = ins
            z = Ids(meta_ref, dims).dp
            for i in range(2):
                chunk = 2 * i + 1 - lax.rem(z, 2)
                outs[i] = (part(value, chunk) + part(other, chunk)).astype(BF16)

        sent = run(f"{self.name}_a", first, self.meta, (self.value, self.other), arr((2, count, rows, cols)))
        near = self.permute(sent, 1)

        def second(meta_ref, ins, outs):
            value, other, near = ins
            chunk = Ids(meta_ref, dims).dp ^ 2
            total = part(value, chunk) + part(other, chunk) + near[lax.div(chunk, 2)].astype(F32)
            outs[...] = total.astype(BF16)

        sent = run(f"{self.name}_b", second, self.meta, (self.value, self.other, near), arr((count, rows, cols)))
        self.pieces = (self.value, self.other, near, self.permute(sent, 2))

    def total(self, ids, pieces, index):
        if self.dims.dp != 4:
            return pieces[index].astype(F32)
        value, other, near, far = pieces
        start = pl.multiple_of(ids.dp * self.rows, 16)
        return (
            value[index, pl.ds(start, self.rows), :].astype(F32)
            + other[index, pl.ds(start, self.rows), :].astype(F32)
            + near[lax.div(ids.dp, 2), index].astype(F32)
            + far[index].astype(F32)
        )

    def operands(self):
        return self.pieces if self.dims.dp == 4 else self.direct


def finish(dims, meta, sums, kinds, name):
    rows = sums[0].rows
    outs = [arr((TYPES, hi - lo, rows) if flip else (TYPES, rows, hi - lo), F32) for _, lo, hi, flip in kinds]

    def body(meta_ref, ins, outs):
        ids = Ids(meta_ref, dims)

        def go(layer):
            for out, (base, lo, hi, flip) in zip(outs, kinds):
                for kind in range(TYPES):
                    total = sums[layer].total(ids, ins[layer], base + kind)[:, lo:hi]
                    out[kind] = total.T if flip else total

        for layer in range(LAYERS):
            pl.when(ids.section == layer)(functools.partial(go, layer))

    return run(name, body, meta, [s.operands() for s in sums], outs, 0, 24)


def small_total(value, axes):
    for axis in axes:
        bit = 1
        while bit < lax.axis_size(axis):
            value = value + swap(value, axis, bit)
            bit *= 2
    return value


def body(
    tokens,
    cotangent,
    lengths,
    chain_type,
    qkv_weight,
    qkv_bias,
    out_weight,
    out_bias,
    ffn_in,
    ffn_in_bias,
    ffn_out,
    ffn_out_bias,
    norm_gain,
    norm_bias,
):
    dims = Dims()
    dims.per_chip, dims.length, dims.d = tokens.shape
    dims.slots = lax.axis_size("tensor")
    dims.dp = lax.axis_size("dp")
    dims.group = lengths.shape[0]
    dims.width = qkv_weight.shape[-1]
    dims.hidden = ffn_in.shape[-1]
    dims.r = dims.length // SPLIT
    sections = lax.axis_size("section")
    assert dims.per_chip == sections == LAYERS and dims.slots & (dims.slots - 1) == 0
    assert dims.dp & (dims.dp - 1) == 0 and 4 * dims.width == dims.d == dims.hidden
    r, d, width = dims.r, dims.d, dims.width
    section = lax.axis_index("section")
    meta = jnp.concatenate(
        [
            jnp.stack([section, lax.axis_index("tensor"), lax.axis_index("dp")]).astype(jnp.int32),
            chain_type,
            lengths,
        ]
    )
    first = section == 0

    def halves(value):
        return [value[h * r : (h + 1) * r] for h in range(SPLIT)]

    own_rows = halves(jnp.where(first, tokens[0], tokens[1]))
    own_cot = halves(jnp.where(first, cotangent[0], cotangent[1]))
    rows = [gather(own_rows[h], dims.slots) for h in range(SPLIT)]

    padded = jnp.concatenate(
        [
            qkv_bias[0, :, 0],
            jnp.zeros_like(qkv_bias[0, :, 0]),
            qkv_bias[0, :, 1],
            jnp.zeros_like(qkv_bias[0, :, 0]),
        ],
        axis=-1,
    )
    packed = jnp.concatenate(
        [
            out_bias[0],
            ffn_out_bias[0],
            norm_gain[0, :, 0],
            norm_gain[0, :, 1],
            norm_bias[0, :, 0],
            norm_bias[0, :, 1],
            ffn_in_bias[0],
            padded,
        ],
        axis=0,
    )
    qkv_own = qkv_weight[0].reshape(TYPES, d, 3 * width)
    weights = [qkv_own, out_weight[0], ffn_in[0], ffn_out[0]]
    swapped = [swap(weight, "section", 1) for weight in weights]
    packed_other = swap(packed, "section", 1)

    def order(meta_ref, ins, outs):
        here = meta_ref[0] == 0
        own, other = ins[0][...], ins[1][...]
        outs[0][...] = jnp.where(here, own, other)
        outs[1][...] = jnp.where(here, other, own)

    small = run("params", order, meta, [packed, packed_other], [arr(packed.shape, F32)] * 2)
    attn_own, attn_other = tuple(weights[:2]), tuple(swapped[:2])
    ffn_own, ffn_other = tuple(weights[2:]), tuple(swapped[2:])
    span = range(SPLIT)

    saved = []
    acts = []
    for layer in range(LAYERS):
        parts, qkv, att = attention_forward(dims, layer, meta, rows, attn_own, attn_other, small[layer])
        parts = [scatter(parts[h]) for h in span]
        firsts = [first_norm(dims, layer, meta, own_rows[h], parts[h], small[layer]) for h in span]
        normed = [gather(firsts[h][0], dims.slots) for h in span]
        ffn = [ffn_forward(dims, layer, meta, normed[h], ffn_own, ffn_other, small[layer]) for h in span]
        parts = [scatter(ffn[h][0]) for h in span]
        if layer < LAYERS - 1:
            seconds = [second_norm(dims, layer, meta, firsts[h][1], parts[h], small[layer]) for h in span]
        else:
            seconds = [
                last_norm(dims, layer, meta, firsts[h][1], parts[h], small[layer], own_cot[h]) for h in span
            ]
        saved.append((rows, qkv, att, firsts, normed, ffn, seconds))
        own_rows = [seconds[h][0] for h in span]
        acts.append(jnp.concatenate(own_rows, axis=0) if SPLIT > 1 else own_rows[0])
        if layer < LAYERS - 1:
            rows = [gather(own_rows[h], dims.slots) for h in span]

    grad_parts = [seconds[h][1:] for h in span]
    input_grads = [None] * LAYERS
    ffn_sums, attn_sums = [None] * LAYERS, [None] * LAYERS
    norm_sums = [None] * LAYERS
    biases = [None] * LAYERS
    for layer in reversed(range(LAYERS)):
        rows, qkv, att, firsts, normed, ffn, seconds = saved[layer]
        second_grad = [grad_parts[h][0] for h in span]
        grads = [gather(grad_parts[h][1], dims.slots) for h in span]
        back = [ffn_backward(dims, layer, meta, grads[h], ffn[h][2], ffn_own, ffn_other) for h in span]
        parts = [scatter(back[h][0]) for h in span]
        ffn_grad, in_bias_grad = ffn_weights(
            dims,
            layer,
            meta,
            normed,
            [[b[1][k] for k in range(dims.slots)] for b in back] if False else [b[1] for b in back],
            grads,
            [f[1] for f in ffn],
        )
        ffn_sums[layer] = GradSum(dims, layer, meta, ffn_grad, f"ffn_sum{layer}")
        ones = [
            first_back(dims, layer, meta, parts[h], second_grad[h], firsts[h][1], firsts[h][2], small[layer])
            for h in span
        ]
        norm_sums[layer] = ([o[2] for o in ones], [grad_parts[h][2] for h in span])
        grads = [gather(ones[h][1], dims.slots) for h in span]
        parts, dqkv = attention_backward(dims, layer, meta, grads, qkv, attn_own, attn_other)
        parts = [scatter(parts[h]) for h in span]
        attn_grad, qkv_bias_grad = attention_weights(dims, layer, meta, rows, dqkv, grads, att)
        attn_sums[layer] = GradSum(dims, layer, meta, attn_grad, f"attn_sum{layer}")
        biases[layer] = (qkv_bias_grad, in_bias_grad)
        if layer > 0:
            seconds = saved[layer - 1][6]
            results = [
                between_layers(
                    dims, layer, meta, parts[h], ones[h][0], seconds[h][1], seconds[h][2], small[layer - 1]
                )
                for h in span
            ]
            input_grads[layer] = [o[0] for o in results]
            grad_parts = [o[1:] for o in results]
        else:
            input_grads[layer] = [input_gradient(dims, layer, meta, parts[h], ones[h][0]) for h in span]

    def collect(meta_ref, ins, outs):
        ids = Ids(meta_ref, dims)
        kind = ids.kind(0)
        for place, layer in ((outs[0], ids.section), (outs[1], 1 - ids.section)):

            def put(which, place=place):
                ones, twos = ins[which]
                one = sum(ref[...] for ref in ones)
                two = sum(ref[...] for ref in twos)
                for t in range(TYPES):
                    here = kind == t
                    place[8 * t : 8 * t + 3, :] = jnp.where(here, one[:3], 0.0)
                    place[8 * t + 3 : 8 * t + 6, :] = jnp.where(here, two[:3], 0.0)
                    place[8 * t + 6 : 8 * t + 8, :] = jnp.zeros((2, d), F32)

            for which in range(LAYERS):
                pl.when(layer == which)(functools.partial(put, which))

    kept, sent = run("norm_sums", collect, meta, norm_sums, [arr((8 * TYPES, d), F32)] * 2)
    norm_total = small_total(kept + swap(sent, "section", 1), ("dp", "tensor"))
    norm_total = norm_total.reshape(TYPES, 8, d)

    def collect_bias(meta_ref, ins, outs):
        here = meta_ref[0] == 0
        for i in range(2):
            zero, one = ins[0][i][...], ins[1][i][...]
            outs[0][2 * i : 2 * i + 2, :] = jnp.where(here, zero, one)
            outs[1][2 * i : 2 * i + 2, :] = jnp.where(here, one, zero)

    kept, sent = run("bias_sums", collect_bias, meta, biases, [arr((2 * TYPES, d), F32)] * 2)
    bias_total = small_total(kept + swap(sent, "section", 1), ("dp",))

    in_total, back_total = finish(
        dims, meta, ffn_sums, [(0, 0, dims.hidden, False), (TYPES, 0, dims.hidden, True)], "ffn_finish"
    )
    qkv_total, out_total = finish(
        dims, meta, attn_sums, [(0, 0, 3 * width, False), (0, 3 * width, 4 * width, True)], "attn_finish"
    )

    def exchange(values):
        received = swap(jnp.where(first, values[1], values[0]), "section", 1)
        return jnp.stack([jnp.where(first, values[0], received), jnp.where(first, received, values[1])])

    acts_out = exchange(acts)
    grads_out = exchange([jnp.concatenate(g, axis=0) for g in input_grads])
    return (
        acts_out[None],
        grads_out[None],
        qkv_total.reshape(1, TYPES, -1, 3, width),
        bias_total[:TYPES, : 3 * width].reshape(TYPES, 3, width)[None, :, ::2],
        out_total[None],
        norm_total[None, :, 2],
        in_total[None],
        bias_total[None, TYPES:],
        back_total[None],
        norm_total[None, :, 5],
        jnp.stack([norm_total[:, 0], norm_total[:, 3]], axis=1)[None],
        jnp.stack([norm_total[:, 1], norm_total[:, 4]], axis=1)[None],
    )


def solution(mesh):
    placed = (
        P(("dp", "tensor"), None, None),
        P(("dp", "tensor"), None, None),
        P("dp"),
        P("dp"),
        P("section", None, None, None, "tensor"),
        P("section", None, None, "tensor"),
        P("section", None, "tensor", None),
        P("section", None, None),
        P("section", None, None, "tensor"),
        P("section", None, "tensor"),
        P("section", None, "tensor", None),
        P("section", None, None),
        P("section", None, None, None),
        P("section", None, None, None),
    )
    return jax.shard_map(
        body,
        mesh=mesh,
        in_specs=placed,
        out_specs=(
            P("section", ("dp", "tensor"), None, None),
            P("section", ("dp", "tensor"), None, None),
            P("section", None, "dp", None, "tensor"),
            P("section", None, None, "tensor"),
            P("section", None, "tensor", "dp"),
            P("section", None, None),
            P("section", None, "dp", "tensor"),
            P("section", None, "tensor"),
            P("section", None, "tensor", "dp"),
            P("section", None, None),
            P("section", None, None, None),
            P("section", None, None, None),
        ),
        check_vma=False,
    )
```

time: 1020 us -> 494 us (0.48)
  blocking collectives: 353 us -> 0 us
  matrix products: 225 us -> 0 us
  Pallas kernels: 0 us -> 93.3 us
  starting transfers between devices: 9.12 us -> 97.8 us
  other arithmetic: 93.4 us -> 6.51 us
  local copies, waits for them, and re-layouts: 124 us -> 42.5 us
  waiting for transfers between devices: 187 us -> 243 us
  between operations: 19.4 us -> 1.83 us
    all_gather x18 -> x0, blocking collectives: 259 us -> none  [the longest x6 86.7 us: forward(): full_rows = lax.all_gather(own_rows, 'tensor', axis=0, tiled=True)]
    ppermute x4 -> x75, waiting for transfers between devices: 1.88 us -> 243 us  [the longest x63 194 us: swap(): lax.ppermute(value, axis, [(source, source ^ bit) for source in range(cou...]
    dot_general x146 -> x0, matrix products: 211 us -> none  [the longest x72 109 us: apply_typed(): jnp.einsum(spec, row_mask(onehot, type_index, rows), table[type_index], p...]
    unnamed x43 -> x0, waiting for transfers between devices: 162 us -> none
    psum x2 -> x0, blocking collectives: 93.9 us -> none  [the longest x1 74.5 us: body(): shard_sums = lax.psum(shard_total, ('dp', 'tensor'))]
    pallas_call x0 -> x33, Pallas kernels: none -> 93.3 us  [run(): pl.pallas_call(kernel, name=name, in_specs=[pl.BlockSpec(memory_space=plt...]
    ppermute x4 -> x75, starting transfers between devices: 7.82 us -> 97.8 us  [the longest x63 74.9 us: swap(): lax.ppermute(value, axis, [(source, source ^ bit) for source in range(cou...]
    reduce_sum x37 -> x0, other arithmetic: 44.9 us -> none  [the longest x11 14.7 us: layer_norm(): center = values - jnp.mean(values, axis=-1, keepdims=True)]
  transfers between devices with their start and end apart: 26 -> 75, of which waited for: 13 -> 45; matrix products, arithmetic and copies ran while one was open for 35% -> 5% of each run, Pallas kernels for 0% -> 11%
where the time goes in v1:
time: 494 us; the launch traced here: 485 us
  waiting for transfers between devices  243 us (49%)
  starting transfers between devices  97.8 us (20%)
  Pallas kernels  93.3 us (19%)
  local copies, waits for them, and re-layouts  42.5 us (9%)
  other arithmetic  6.51 us (1%)
    ppermute x63, waiting for transfers between devices, swap(): lax.ppermute(value, axis, [(source, source ^ bit) for source in range(cou...  194 us
    pallas_call x33, Pallas kernels, run(): pl.pallas_call(kernel, name=name, in_specs=[pl.BlockSpec(memory_space=plt...  93.3 us
    ppermute x63, starting transfers between devices, swap(): lax.ppermute(value, axis, [(source, source ^ bit) for source in range(cou...  74.9 us
    ppermute x8, waiting for transfers between devices, permute(): return lax.ppermute(value, ('section', 'dp'), pairs)  48.9 us
    unnamed x86, local copies, waits for them, and re-layouts  26.3 us
    ppermute x8, starting transfers between devices, permute(): return lax.ppermute(value, ('section', 'dp'), pairs)  17.1 us
  transfers between devices with their start and end apart: 75, of which 45 were waited for; matrix products, arithmetic and copies ran while one was open for 5% of the time, Pallas kernels for 11%

profile of v1, /device:TPU:0, one launch (start us, length us, event | category | flops | bytes accessed | tf_op | source)
XLA Modules:
  0.0 485.2 jit_solution(2330180440623678029)
XLA Ops:
  12.5 6.3 %collective-permute-done.2.refs_3_ = bf16[160,768]{1,0:T(8,128)(2,1)S(1)} collective-permute-done((bf16[160,768]{1,0:T(8,128)(2,1)S(1)}, bf16[160,768]{1,0:T(8,128)(2,1)S(1)}, u32[]{:S(2)}, u32[]{:S(2)}) %collective-permute-start.2) | collective-permute-done | bytes 245792 | tf_op jit(solution)/shard_map/ppermute | solution.py:417
  34.6 5.4 %attn_fwd0.1 = (bf16[160,768]{1,0:T(8,128)(2,1)S(1)}, bf16[160,768]{1,0:T(8,128)(2,1)S(1)}, bf16[160,768]{1,0:T(8,128)(2,1)S(1)}, bf16[160,768]{1,0:T(8,128)(2,1...) custom-call(s32[19]{0:T(128)S(1)} %concatenate.9.meta_ref, ...), custom_call_target="tpu_custom_call" | custom-call | flops 754974720 | bytes 7716864 | tf_op jit(solution)/shard_map/attn_fwd0/pallas_call | solution.py:52
  43.6 5.4 %collective-permute-done.6.refs_2_ = bf16[160,768]{1,0:T(8,128)(2,1)S(1)} collective-permute-done((bf16[160,768]{1,0:T(8,128)(2,1)S(1)}, bf16[160,768]{1,0:T(8,128)(2,1)S(1)}, u32[]{:S(2)}, u32[]{:S(2)}) %collective-permute-start.6) | collective-permute-done | bytes 245792 | tf_op jit(solution)/shard_map/ppermute | solution.py:417
  56.7 5.6 %collective-permute-done.11.refs_3_ = bf16[160,768]{1,0:T(8,128)(2,1)S(1)} collective-permute-done((bf16[160,768]{1,0:T(8,128)(2,1)S(1)}, bf16[160,768]{1,0:T(8,128)(2,1)S(1)}, u32[]{:S(2)}, u32[]{:S(2)}) %collective-permute-start.11) | collective-permute-done | bytes 245792 | tf_op jit(solution)/shard_map/ppermute | solution.py:417
  64.9 5.5 %ffn_fwd0.1 = (bf16[160,768]{1,0:T(8,128)(2,1)S(1)}, bf16[160,768]{1,0:T(8,128)(2,1)S(1)}, bf16[160,768]{1,0:T(8,128)(2,1)S(1)}, bf16[160,768]{1,0:T(8,128)(2,1)...) custom-call(s32[19]{0:T(128)S(1)} %concatenate.9.meta_ref, ...), custom_call_target="tpu_custom_call" | custom-call | flops 1509949440 | bytes 13418496 | tf_op jit(solution)/shard_map/ffn_fwd0/pallas_call | solution.py:52
  74.0 5.4 %collective-permute-done.14.refs_2_ = bf16[160,768]{1,0:T(8,128)(2,1)S(1)} collective-permute-done((bf16[160,768]{1,0:T(8,128)(2,1)S(1)}, bf16[160,768]{1,0:T(8,128)(2,1)S(1)}, u32[]{:S(2)}, u32[]{:S(2)}) %collective-permute-start.14) | collective-permute-done | bytes 245792 | tf_op jit(solution)/shard_map/ppermute | solution.py:417
  87.6 5.9 %collective-permute-done.19.refs_3_ = bf16[160,768]{1,0:T(8,128)(2,1)S(1)} collective-permute-done((bf16[160,768]{1,0:T(8,128)(2,1)S(1)}, bf16[160,768]{1,0:T(8,128)(2,1)S(1)}, u32[]{:S(2)}, u32[]{:S(2)}) %collective-permute-start.19) | collective-permute-done | bytes 245792 | tf_op jit(solution)/shard_map/ppermute | solution.py:417
  95.5 4.8 attn_fwd1.1
  103.9 5.4 %collective-permute-done.20.refs_2_ = bf16[160,768]{1,0:T(8,128)(2,1)S(1)} collective-permute-done((bf16[160,768]{1,0:T(8,128)(2,1)S(1)}, bf16[160,768]{1,0:T(8,128)(2,1)S(1)}, u32[]{:S(2)}, u32[]{:S(2)}) %collective-permute-start.20) | collective-permute-done | bytes 245792 | tf_op jit(solution)/shard_map/ppermute | solution.py:417
  109.3 4.6 collective-permute-done.21.refs_3_
  118.3 5.6 %collective-permute-done.25.refs_3_ = bf16[160,768]{1,0:T(8,128)(2,1)S(1)} collective-permute-done((bf16[160,768]{1,0:T(8,128)(2,1)S(1)}, bf16[160,768]{1,0:T(8,128)(2,1)S(1)}, u32[]{:S(2)}, u32[]{:S(2)}) %collective-permute-start.25) | collective-permute-done | bytes 245792 | tf_op jit(solution)/shard_map/ppermute | solution.py:417
  126.4 5.1 %ffn_fwd1.1 = (bf16[160,768]{1,0:T(8,128)(2,1)S(1)}, bf16[160,768]{1,0:T(8,128)(2,1)S(1)}, bf16[160,768]{1,0:T(8,128)(2,1)S(1)}, bf16[160,768]{1,0:T(8,128)(2,1)...) custom-call(s32[19]{0:T(128)S(1)} %concatenate.9.meta_ref, ...), custom_call_target="tpu_custom_call" | custom-call | flops 1509949440 | bytes 13418496 | tf_op jit(solution)/shard_map/ffn_fwd1/pallas_call | solution.py:52
  135.1 5.4 %collective-permute-done.26.refs_2_ = bf16[160,768]{1,0:T(8,128)(2,1)S(1)} collective-permute-done((bf16[160,768]{1,0:T(8,128)(2,1)S(1)}, bf16[160,768]{1,0:T(8,128)(2,1)S(1)}, u32[]{:S(2)}, u32[]{:S(2)}) %collective-permute-start.26) | collective-permute-done | bytes 245792 | tf_op jit(solution)/shard_map/ppermute | solution.py:417
  149.0 6.1 %collective-permute-done.32.refs_3_.refs_8_ = bf16[160,768]{1,0:T(8,128)(2,1)S(1)} collective-permute-done((bf16[160,768]{1,0:T(8,128)(2,1)S(1)}, bf16[160,768]{1,0:T(8,128)(2,1)S(1)}, u32[]{:S(2)}, u32[]{:S(2)}) %collective-permute-start.32) | collective-permute-done | bytes 245792 | tf_op jit(solution)/shard_map/ppermute | solution.py:417
  157.7 5.3 %ffn_bwd1.1 = (bf16[160,768]{1,0:T(8,128)(2,1)S(1)}, bf16[160,768]{1,0:T(8,128)(2,1)S(1)}, bf16[160,768]{1,0:T(8,128)(2,1)S(1)}, bf16[160,768]{1,0:T(8,128)(2,1)S(1)}, bf16[4,160,768]{2,1,0:T(8,128)(2,1)S(1)}) custom-call(s32[19]{0:T(128)S(1)} %concatenate.9.meta_ref, bf16[160,768]{1,0:T(8,128)(2,1)S(1)} %get-tuple-element.121.refs_0_.refs_5_, ...), custom_call_target="tpu_custom_call" | custom-call | flops 1509949440 | bytes 13369344 | tf_op jit(solution)/shard_map/ffn_bwd1/pallas_call | solution.py:52
  166.6 5.4 %collective-permute-done.33.refs_1_ = bf16[160,768]{1,0:T(8,128)(2,1)S(1)} collective-permute-done((bf16[160,768]{1,0:T(8,128)(2,1)S(1)}, bf16[160,768]{1,0:T(8,128)(2,1)S(1)}, u32[]{:S(2)}, u32[]{:S(2)}) %collective-permute-start.33) | collective-permute-done | bytes 245792 | tf_op jit(solution)/shard_map/ppermute | solution.py:417
  172.0 4.3 collective-permute-done.34.refs_2_
  180.9 5.3 %collective-permute-done.38.refs_3_.refs_8_ = bf16[160,768]{1,0:T(8,128)(2,1)S(1)} collective-permute-done((bf16[160,768]{1,0:T(8,128)(2,1)S(1)}, bf16[160,768]{1,0:T(8,128)(2,1)S(1)}, u32[]{:S(2)}, u32[]{:S(2)}) %collective-permute-start.38) | collective-permute-done | bytes 245792 | tf_op jit(solution)/shard_map/ppermute | solution.py:417
  189.5 9.5 %attn_bwd1.1 = (bf16[160,768]{1,0:T(8,128)(2,1)S(1)}, bf16[160,768]{1,0:T(8,128)(2,1)S(1)}, bf16[160,768]{1,0:T(8,128)(2,1)S(1)}, bf16[160,768]{1,0:T(8,128)(2,1)S(1)}, bf16[4,160,576]{2,1,0:T(8,128)(2,1)S(1)}) custom-call(s32[19]{0:T(128)S(1)} %concatenate.9.meta_ref, bf16[160,768]{1,0:T(8,128)(2,1)S(1)} %get-tuple-element.129.refs_0_.refs_5_, ...), custom_call_target="tpu_custom_call" | custom-call | flops 754974720 | bytes 8159232 | tf_op jit(solution)/shard_map/attn_bwd1/pallas_call | solution.py:52
  202.5 5.4 %collective-permute-done.39.refs_1_ = bf16[160,768]{1,0:T(8,128)(2,1)S(1)} collective-permute-done((bf16[160,768]{1,0:T(8,128)(2,1)S(1)}, bf16[160,768]{1,0:T(8,128)(2,1)S(1)}, u32[]{:S(2)}, u32[]{:S(2)}) %collective-permute-start.39) | collective-permute-done | bytes 245792 | tf_op jit(solution)/shard_map/ppermute | solution.py:417
  207.9 5.3 %collective-permute-done.40.refs_2_ = bf16[160,768]{1,0:T(8,128)(2,1)S(1)} collective-permute-done((bf16[160,768]{1,0:T(8,128)(2,1)S(1)}, bf16[160,768]{1,0:T(8,128)(2,1)S(1)}, u32[]{:S(2)}, u32[]{:S(2)}) %collective-permute-start.40) | collective-permute-done | bytes 245792 | tf_op jit(solution)/shard_map/ppermute | solution.py:417
  217.8 4.4 ffn_dw1.1
  227.0 5.3 %ffn_bwd0.1 = (bf16[160,768]{1,0:T(8,128)(2,1)S(1)}, bf16[160,768]{1,0:T(8,128)(2,1)S(1)}, bf16[160,768]{1,0:T(8,128)(2,1)S(1)}, bf16[160,768]{1,0:T(8,128)(2,1)S(1)}, bf16[4,160,768]{2,1,0:T(8,128)(2,1)S(1)}) custom-call(s32[19]{0:T(128)S(1)} %concatenate.9.meta_ref, bf16[160,768]{1,0:T(8,128)(2,1)S(1)} %get-tuple-element.138.refs_0_.refs_5_, ...), custom_call_target="tpu_custom_call" | custom-call | flops 1509949440 | bytes 13369344 | tf_op jit(solution)/shard_map/ffn_bwd0/pallas_call | solution.py:52
  232.3 4.5 ffn_dw0.1
  241.8 5.0 %collective-permute-done.45.refs_1_ = bf16[160,768]{1,0:T(8,128)(2,1)S(1)} collective-permute-done((bf16[160,768]{1,0:T(8,128)(2,1)S(1)}, bf16[160,768]{1,0:T(8,128)(2,1)S(1)}, u32[]{:S(2)}, u32[]{:S(2)}) %collective-permute-start.45) | collective-permute-done | bytes 245792 | tf_op jit(solution)/shard_map/ppermute | solution.py:417
  247.6 4.7 collective-permute-done.47.refs_3_
  267.7 9.1 %attn_bwd0.1 = (bf16[160,768]{1,0:T(8,128)(2,1)S(1)}, bf16[160,768]{1,0:T(8,128)(2,1)S(1)}, bf16[160,768]{1,0:T(8,128)(2,1)S(1)}, bf16[160,768]{1,0:T(8,128)(2,1)S(1)}, bf16[4,160,576]{2,1,0:T(8,128)(2,1)S(1)}) custom-call(s32[19]{0:T(128)S(1)} %concatenate.9.meta_ref, bf16[160,768]{1,0:T(8,128)(2,1)S(1)} %get-tuple-element.146.refs_0_.refs_5_, ...), custom_call_target="tpu_custom_call" | custom-call | flops 754974720 | bytes 8159232 | tf_op jit(solution)/shard_map/attn_bwd0/pallas_call | solution.py:52
  291.5 49.0 %collective-permute-done.65 = f32[16,768]{1,0:T(8,128)S(1)} collective-permute-done((f32[16,768]{1,0:T(8,128)S(1)}, f32[16,768]{1,0:T(8,128)S(1)}, u32[]{:S(2)}, u32[]{:S(2)}) %collective-permute-start.65) | collective-permute-done | bytes 49184 | tf_op jit(solution)/shard_map/ppermute | solution.py:417
  370.1 4.6 collective-permute-done.53.refs_3_
  387.2 4.4 collective-permute-done.63
  402.9 5.4 %collective-permute-start.57 = (bf16[2,192,768]{2,1,0:T(8,128)(2,1)S(1)}, bf16[2,192,768]{2,1,0:T(8,128)(2,1)S(1)}, u32[]{:S(2)}, u32[]{:S(2)}) collective-permute-start(bf16[2,192,768]{2,1,0:T(8,128)(2,1)S(1)} %attn_sum0_b.1), channel_id=1, source_target_pairs={{0,8},{4,12},{8,0},{12,4},{1,9},{5,13},{9,1},{13,5},{2,10},{6,14},... | collective-permute-start | bytes 1769480 | tf_op jit(solution)/shard_map/ppermute | solution.py:442
  411.2 48.2 %collective-permute-done.57.refs_3_ = bf16[2,192,768]{2,1,0:T(8,128)(2,1)S(1)} collective-permute-done((bf16[2,192,768]{2,1,0:T(8,128)(2,1)S(1)}, bf16[2,192,768]{2,1,0:T(8,128)(2,1)S(1)}, u32[]{:S(2)}, u32[]{:S(2)}) %collective-permute-start.57) | collective-permute-done | bytes 589856 | tf_op jit(solution)/shard_map/ppermute | solution.py:442
  (273 shorter events, 222.0 us)
Async XLA Ops:
  0.6 20.5 %collective-permute-start.3 = (bf16[2,768,576]{1,2,0:T(8,128)(2,1)}, bf16[2,768,576]{1,2,0:T(8,128)(2,1)S(1)}, u32[]{:S(2)}, u32[]{:S(2)}) collective-permute-start(bf16[2,768,576]{1,2,0:T(8,128)(2,1)} %bitcast.74), channel_id=1, source_target_pairs={{0,16},{16,0},{1,17},{17,1},{2,18},{18,2},{3,19},{19,3},{4,20},{20... | collective-permute-start | bytes 5308424 | tf_op jit(solution)/shard_map/ppermute | solution.py:417
  1.2 63.7 %collective-permute-start.12 = (bf16[2,768,768]{2,1,0:T(8,128)(2,1)}, bf16[2,768,768]{2,1,0:T(8,128)(2,1)}, u32[]{:S(2)}, u32[]{:S(2)}) collective-permute-start(bf16[2,768,768]{2,1,0:T(8,128)(2,1)} %bitcast.57), channel_id=1, source_target_pairs={{0,16},{16,0},{1,17},{17,1},{2,18},{18,2},{3,19},{19,3},{4,20},{20... | collective-permute-start | bytes 7077896 | tf_op jit(solution)/shard_map/ppermute | solution.py:417
  1.2 63.6 %collective-permute-start.13 = (bf16[2,768,768]{2,1,0:T(8,128)(2,1)}, bf16[2,768,768]{2,1,0:T(8,128)(2,1)}, u32[]{:S(2)}, u32[]{:S(2)}) collective-permute-start(bf16[2,768,768]{2,1,0:T(8,128)(2,1)} %bitcast.62), channel_id=1, source_target_pairs={{0,16},{16,0},{1,17},{17,1},{2,18},{18,2},{3,19},{19,3},{4,20},{20... | collective-permute-start | bytes 7077896 | tf_op jit(solution)/shard_map/ppermute | solution.py:417
  5.8 26.4 %collective-permute-start.4 = (bf16[2,192,768]{2,1,0:T(8,128)(2,1)}, bf16[2,192,768]{2,1,0:T(8,128)(2,1)S(1)}, u32[]{:S(2)}, u32[]{:S(2)}) collective-permute-start(bf16[2,192,768]{2,1,0:T(8,128)(2,1)} %bitcast.67), channel_id=1, source_target_pairs={{0,16},{16,0},{1,17},{17,1},{2,18},{18,2},{3,19},{19,3},{4,20},{20... | collective-permute-start | bytes 1769480 | tf_op jit(solution)/shard_map/ppermute | solution.py:417
  19.4 12.7 %collective-permute-start.1 = (bf16[160,768]{1,0:T(8,128)(2,1)S(1)}, bf16[160,768]{1,0:T(8,128)(2,1)}, u32[]{:S(2)}, u32[]{:S(2)}) collective-permute-start(bf16[160,768]{1,0:T(8,128)(2,1)S(1)} %select_bitcast_fusion.5.refs_0_), channel_id=1, source_target_pairs={{0,2},{1,3},{2,0},{3,1},{4,6},{5,7},{6,4},{7,5},{8,10},{9,11},{10,... | collective-permute-start | bytes 737288 | tf_op jit(solution)/shard_map/ppermute | solution.py:417
  40.7 11.6 %collective-permute-start.7 = (bf16[160,768]{1,0:T(8,128)(2,1)S(1)}, bf16[160,768]{1,0:T(8,128)(2,1)S(1)}, u32[]{:S(2)}, u32[]{:S(2)}) collective-permute-start(bf16[160,768]{1,0:T(8,128)(2,1)S(1)} %get-tuple-element.100), channel_id=1, source_target_pairs={{0,2},{1,3},{2,0},{3,1},{4,6},{5,7},{6,4},{7,5},{8,10},{9,11},{10,... | collective-permute-start | bytes 737288 | tf_op jit(solution)/shard_map/ppermute | solution.py:417
  41.0 11.3 %collective-permute-start.8 = (bf16[160,768]{1,0:T(8,128)(2,1)S(1)}, bf16[160,768]{1,0:T(8,128)(2,1)S(1)}, u32[]{:S(2)}, u32[]{:S(2)}) collective-permute-start(bf16[160,768]{1,0:T(8,128)(2,1)S(1)} %get-tuple-element.101), channel_id=1, source_target_pairs={{0,3},{1,2},{2,1},{3,0},{4,7},{5,6},{6,5},{7,4},{8,11},{9,10},{10,... | collective-permute-start | bytes 737288 | tf_op jit(solution)/shard_map/ppermute | solution.py:417
  101.8 12.0 %collective-permute-start.21 = (bf16[160,768]{1,0:T(8,128)(2,1)S(1)}, bf16[160,768]{1,0:T(8,128)(2,1)S(1)}, u32[]{:S(2)}, u32[]{:S(2)}) collective-permute-start(bf16[160,768]{1,0:T(8,128)(2,1)S(1)} %get-tuple-element.112), channel_id=1, source_target_pairs={{0,2},{1,3},{2,0},{3,1},{4,6},{5,7},{6,4},{7,5},{8,10},{9,11},{10,... | collective-permute-start | bytes 737288 | tf_op jit(solution)/shard_map/ppermute | solution.py:417
  102.4 11.4 %collective-permute-start.22 = (bf16[160,768]{1,0:T(8,128)(2,1)S(1)}, bf16[160,768]{1,0:T(8,128)(2,1)S(1)}, u32[]{:S(2)}, u32[]{:S(2)}) collective-permute-start(bf16[160,768]{1,0:T(8,128)(2,1)S(1)} %get-tuple-element.113), channel_id=1, source_target_pairs={{0,3},{1,2},{2,1},{3,0},{4,7},{5,6},{6,5},{7,4},{8,11},{9,10},{10,... | collective-permute-start | bytes 737288 | tf_op jit(solution)/shard_map/ppermute | solution.py:417
  132.5 11.8 %collective-permute-start.27 = (bf16[160,768]{1,0:T(8,128)(2,1)S(1)}, bf16[160,768]{1,0:T(8,128)(2,1)S(1)}, u32[]{:S(2)}, u32[]{:S(2)}) collective-permute-start(bf16[160,768]{1,0:T(8,128)(2,1)S(1)} %get-tuple-element.118), channel_id=1, source_target_pairs={{0,2},{1,3},{2,0},{3,1},{4,6},{5,7},{6,4},{7,5},{8,10},{9,11},{10,... | collective-permute-start | bytes 737288 | tf_op jit(solution)/shard_map/ppermute | solution.py:417
  164.3 12.0 %collective-permute-start.34 = (bf16[160,768]{1,0:T(8,128)(2,1)S(1)}, bf16[160,768]{1,0:T(8,128)(2,1)S(1)}, u32[]{:S(2)}, u32[]{:S(2)}) collective-permute-start(bf16[160,768]{1,0:T(8,128)(2,1)S(1)} %get-tuple-element.125), channel_id=1, source_target_pairs={{0,2},{1,3},{2,0},{3,1},{4,6},{5,7},{6,4},{7,5},{8,10},{9,11},{10,... | collective-permute-start | bytes 737288 | tf_op jit(solution)/shard_map/ppermute | solution.py:417
  200.8 12.4 %collective-permute-start.40 = (bf16[160,768]{1,0:T(8,128)(2,1)S(1)}, bf16[160,768]{1,0:T(8,128)(2,1)S(1)}, u32[]{:S(2)}, u32[]{:S(2)}) collective-permute-start(bf16[160,768]{1,0:T(8,128)(2,1)S(1)} %get-tuple-element.133), channel_id=1, source_target_pairs={{0,2},{1,3},{2,0},{3,1},{4,6},{5,7},{6,4},{7,5},{8,10},{9,11},{10,... | collective-permute-start | bytes 737288 | tf_op jit(solution)/shard_map/ppermute | solution.py:417
  201.7 11.5 %collective-permute-start.41 = (bf16[160,768]{1,0:T(8,128)(2,1)S(1)}, bf16[160,768]{1,0:T(8,128)(2,1)S(1)}, u32[]{:S(2)}, u32[]{:S(2)}) collective-permute-start(bf16[160,768]{1,0:T(8,128)(2,1)S(1)} %get-tuple-element.134), channel_id=1, source_target_pairs={{0,3},{1,2},{2,1},{3,0},{4,7},{5,6},{6,5},{7,4},{8,11},{9,10},{10,... | collective-permute-start | bytes 737288 | tf_op jit(solution)/shard_map/ppermute | solution.py:417
  215.8 11.2 %collective-permute-start.43 = (bf16[160,768]{1,0:T(8,128)(2,1)S(1)}, bf16[160,768]{1,0:T(8,128)(2,1)S(1)}, u32[]{:S(2)}, u32[]{:S(2)}) collective-permute-start(bf16[160,768]{1,0:T(8,128)(2,1)S(1)} %get-tuple-element.138.refs_0_.refs_5_), channel_id=1, source_target_pairs={{0,2},{1,3},{2,0},{3,1},{4,6},{5,7},{6,4},{7,5},{8,10},{9,11},{10,... | collective-permute-start | bytes 737288 | tf_op jit(solution)/shard_map/ppermute | solution.py:417
  216.1 10.9 %collective-permute-start.42 = (bf16[160,768]{1,0:T(8,128)(2,1)S(1)}, bf16[160,768]{1,0:T(8,128)(2,1)S(1)}, u32[]{:S(2)}, u32[]{:S(2)}) collective-permute-start(bf16[160,768]{1,0:T(8,128)(2,1)S(1)} %get-tuple-element.138.refs_0_.refs_5_), channel_id=1, source_target_pairs={{0,1},{1,0},{2,3},{3,2},{4,5},{5,4},{6,7},{7,6},{8,9},{9,8},{10,11... | collective-permute-start | bytes 737288 | tf_op jit(solution)/shard_map/ppermute | solution.py:417
  222.2 59.7 %collective-permute-start.72 = (bf16[4,768,768]{2,1,0:T(8,128)(2,1)S(1)}, bf16[4,768,768]{2,1,0:T(8,128)(2,1)S(1)}, u32[]{:S(2)}, u32[]{:S(2)}) collective-permute-start(bf16[4,768,768]{2,1,0:T(8,128)(2,1)S(1)} %get-tuple-element.179.refs_0_.refs_4_), channel_id=1, source_target_pairs={{0,16},{1,17},{2,18},{3,19},{4,20},{5,21},{6,22},{7,23},{8,24},{9,... | collective-permute-start | bytes 14155784 | tf_op jit(solution)/shard_map/ppermute | solution.py:432
  236.8 47.1 %collective-permute-start.69 = (bf16[4,768,768]{2,1,0:T(8,128)(2,1)S(1)}, bf16[4,768,768]{2,1,0:T(8,128)(2,1)S(1)}, u32[]{:S(2)}, u32[]{:S(2)}) collective-permute-start(bf16[4,768,768]{2,1,0:T(8,128)(2,1)S(1)} %get-tuple-element.178.refs_0_), channel_id=1, source_target_pairs={{16,0},{17,1},{18,2},{19,3},{20,4},{21,5},{22,6},{23,7},{24,8},{25... | collective-permute-start | bytes 14155784 | tf_op jit(solution)/shard_map/ppermute | solution.py:432
  240.1 12.2 %collective-permute-start.47 = (bf16[160,768]{1,0:T(8,128)(2,1)S(1)}, bf16[160,768]{1,0:T(8,128)(2,1)S(1)}, u32[]{:S(2)}, u32[]{:S(2)}) collective-permute-start(bf16[160,768]{1,0:T(8,128)(2,1)S(1)} %get-tuple-element.143), channel_id=1, source_target_pairs={{0,3},{1,2},{2,1},{3,0},{4,7},{5,6},{6,5},{7,4},{8,11},{9,10},{10,... | collective-permute-start | bytes 737288 | tf_op jit(solution)/shard_map/ppermute | solution.py:417
  255.5 12.2 %collective-permute-start.49 = (bf16[160,768]{1,0:T(8,128)(2,1)S(1)}, bf16[160,768]{1,0:T(8,128)(2,1)S(1)}, u32[]{:S(2)}, u32[]{:S(2)}) collective-permute-start(bf16[160,768]{1,0:T(8,128)(2,1)S(1)} %get-tuple-element.146.refs_0_.refs_5_), channel_id=1, source_target_pairs={{0,2},{1,3},{2,0},{3,1},{4,6},{5,7},{6,4},{7,5},{8,10},{9,11},{10,... | collective-permute-start | bytes 737288 | tf_op jit(solution)/shard_map/ppermute | solution.py:417
  263.1 91.0 %collective-permute-start.58 = (bf16[2,768,768]{2,1,0:T(8,128)(2,1)S(1)}, bf16[2,768,768]{2,1,0:T(8,128)(2,1)S(1)}, u32[]{:S(2)}, u32[]{:S(2)}) collective-permute-start(bf16[2,768,768]{2,1,0:T(8,128)(2,1)S(1)} %get-tuple-element.159.refs_0_.refs_4_), channel_id=1, source_target_pairs={{0,16},{1,17},{2,18},{3,19},{4,20},{5,21},{6,22},{7,23},{8,24},{9,... | collective-permute-start | bytes 7077896 | tf_op jit(solution)/shard_map/ppermute | solution.py:432
  280.6 74.4 %collective-permute-start.55 = (bf16[2,768,768]{2,1,0:T(8,128)(2,1)S(1)}, bf16[2,768,768]{2,1,0:T(8,128)(2,1)S(1)}, u32[]{:S(2)}, u32[]{:S(2)}) collective-permute-start(bf16[2,768,768]{2,1,0:T(8,128)(2,1)S(1)} %get-tuple-element.156.refs_0_), channel_id=1, source_target_pairs={{16,0},{17,1},{18,2},{19,3},{20,4},{21,5},{22,6},{23,7},{24,8},{25... | collective-permute-start | bytes 7077896 | tf_op jit(solution)/shard_map/ppermute | solution.py:432
  283.1 95.7 %collective-permute-start.73 = (bf16[2,4,192,768]{3,2,1,0:T(8,128)(2,1)S(1)}, bf16[2,4,192,768]{3,2,1,0:T(8,128)(2,1)S(1)}, u32[]{:S(2)}, u32[]{:S(2)}) collective-permute-start(bf16[2,4,192,768]{3,2,1,0:T(8,128)(2,1)S(1)} %ffn_sum1_a.1), channel_id=1, source_target_pairs={{16,20},{20,16},{24,28},{28,24},{17,21},{21,17},{25,29},{29,25},{1... | collective-permute-start | bytes 7077896 | tf_op jit(solution)/shard_map/ppermute | solution.py:442
  285.0 97.4 %collective-permute-start.70 = (bf16[2,4,192,768]{3,2,1,0:T(8,128)(2,1)S(1)}, bf16[2,4,192,768]{3,2,1,0:T(8,128)(2,1)S(1)}, u32[]{:S(2)}, u32[]{:S(2)}) collective-permute-start(bf16[2,4,192,768]{3,2,1,0:T(8,128)(2,1)S(1)} %ffn_sum0_a.1), channel_id=1, source_target_pairs={{0,4},{4,0},{8,12},{12,8},{1,5},{5,1},{9,13},{13,9},{2,6},{6,2},{1... | collective-permute-start | bytes 7077896 | tf_op jit(solution)/shard_map/ppermute | solution.py:442
  290.9 49.5 %collective-permute-start.65 = (f32[16,768]{1,0:T(8,128)S(1)}, f32[16,768]{1,0:T(8,128)S(1)}, u32[]{:S(2)}, u32[]{:S(2)}) collective-permute-start(f32[16,768]{1,0:T(8,128)S(1)} %add.27), channel_id=1, source_target_pairs={{0,4},{4,0},{8,12},{12,8},{1,5},{5,1},{9,13},{13,9},{2,6},{6,2},{1... | collective-permute-start | bytes 147464 | tf_op jit(solution)/shard_map/ppermute | solution.py:417
  361.8 35.6 %collective-permute-start.59 = (bf16[2,2,192,768]{3,2,1,0:T(8,128)(2,1)}, bf16[2,2,192,768]{3,2,1,0:T(8,128)(2,1)S(1)}, u32[]{:S(2)}, u32[]{:S(2)}) collective-permute-start(bf16[2,2,192,768]{3,2,1,0:T(8,128)(2,1)} %attn_sum1_a.1), channel_id=1, source_target_pairs={{16,20},{20,16},{24,28},{28,24},{17,21},{21,17},{25,29},{29,25},{1... | collective-permute-start | bytes 3538952 | tf_op jit(solution)/shard_map/ppermute | solution.py:442
  362.5 38.8 %collective-permute-start.56 = (bf16[2,2,192,768]{3,2,1,0:T(8,128)(2,1)}, bf16[2,2,192,768]{3,2,1,0:T(8,128)(2,1)}, u32[]{:S(2)}, u32[]{:S(2)}) collective-permute-start(bf16[2,2,192,768]{3,2,1,0:T(8,128)(2,1)} %attn_sum0_a.1), channel_id=1, source_target_pairs={{0,4},{4,0},{8,12},{12,8},{1,5},{5,1},{9,13},{13,9},{2,6},{6,2},{1... | collective-permute-start | bytes 3538952 | tf_op jit(solution)/shard_map/ppermute | solution.py:442
  374.7 16.9 %collective-permute-start.63 = (f32[4,768]{1,0:T(4,128)S(1)}, f32[4,768]{1,0:T(4,128)S(1)}, u32[]{:S(2)}, u32[]{:S(2)}) collective-permute-start(f32[4,768]{1,0:T(4,128)S(1)} %add.25), channel_id=1, source_target_pairs={{0,8},{4,12},{8,0},{12,4},{1,9},{5,13},{9,1},{13,5},{2,10},{6,14},... | collective-permute-start | bytes 36872 | tf_op jit(solution)/shard_map/ppermute | solution.py:417
  380.7 85.5 %collective-permute-start.74 = (bf16[4,192,768]{2,1,0:T(8,128)(2,1)}, bf16[4,192,768]{2,1,0:T(8,128)(2,1)}, u32[]{:S(2)}, u32[]{:S(2)}) collective-permute-start(bf16[4,192,768]{2,1,0:T(8,128)(2,1)} %ffn_sum1_b.1), channel_id=1, source_target_pairs={{16,24},{20,28},{24,16},{28,20},{17,25},{21,29},{25,17},{29,21},{1... | collective-permute-start | bytes 3538952 | tf_op jit(solution)/shard_map/ppermute | solution.py:442
  384.4 81.8 %collective-permute-start.71 = (bf16[4,192,768]{2,1,0:T(8,128)(2,1)}, bf16[4,192,768]{2,1,0:T(8,128)(2,1)}, u32[]{:S(2)}, u32[]{:S(2)}) collective-permute-start(bf16[4,192,768]{2,1,0:T(8,128)(2,1)} %ffn_sum0_b.1), channel_id=1, source_target_pairs={{0,8},{4,12},{8,0},{12,4},{1,9},{5,13},{9,1},{13,5},{2,10},{6,14},... | collective-permute-start | bytes 3538952 | tf_op jit(solution)/shard_map/ppermute | solution.py:442
  391.6 17.3 %collective-permute-start.54 = (f32[160,768]{1,0:T(8,128)}, f32[160,768]{1,0:T(8,128)}, u32[]{:S(2)}, u32[]{:S(2)}) collective-permute-start(f32[160,768]{1,0:T(8,128)} %broadcast_select_fusion), channel_id=1, source_target_pairs={{0,16},{16,0},{1,17},{17,1},{2,18},{18,2},{3,19},{19,3},{4,20},{20... | collective-permute-start | bytes 1474568 | tf_op jit(solution)/shard_map/ppermute | solution.py:417
  399.8 11.4 %collective-permute-start.60 = (bf16[2,192,768]{2,1,0:T(8,128)(2,1)S(1)}, bf16[2,192,768]{2,1,0:T(8,128)(2,1)S(1)}, u32[]{:S(2)}, u32[]{:S(2)}) collective-permute-start(bf16[2,192,768]{2,1,0:T(8,128)(2,1)S(1)} %attn_sum1_b.1), channel_id=1, source_target_pairs={{16,24},{20,28},{24,16},{28,20},{17,25},{21,29},{25,17},{29,21},{1... | collective-permute-start | bytes 1769480 | tf_op jit(solution)/shard_map/ppermute | solution.py:442
  402.9 56.5 %collective-permute-start.57 = (bf16[2,192,768]{2,1,0:T(8,128)(2,1)S(1)}, bf16[2,192,768]{2,1,0:T(8,128)(2,1)S(1)}, u32[]{:S(2)}, u32[]{:S(2)}) collective-permute-start(bf16[2,192,768]{2,1,0:T(8,128)(2,1)S(1)} %attn_sum0_b.1), channel_id=1, source_target_pairs={{0,8},{4,12},{8,0},{12,4},{1,9},{5,13},{9,1},{13,5},{2,10},{6,14},... | collective-permute-start | bytes 1769480 | tf_op jit(solution)/shard_map/ppermute | solution.py:442
  (84 other events, 1501.4 us)

commit v2 on v1

v2 whole, which is shorter than its diff:
```python
import functools
import math

import jax
import jax.numpy as jnp
from jax import lax
from jax.experimental import pallas as pl
from jax.experimental.pallas import tpu as pltpu
from jax.sharding import PartitionSpec as P

HEAD_DIM = 64
TYPES = 2
LAYERS = 2
EPS = 1e-06
HALF_ROOT = 0.7071067811865476
DENSITY = 0.3989422804014327
SCALE = 1.0 / math.sqrt(HEAD_DIM)
MIB = 1 << 20

F32 = jnp.float32
BF16 = jnp.bfloat16

TAIL = 16
FIRST_SUMS, SECOND_SUMS, QKV_SUMS, IN_SUMS, SMALL = 0, 6, 12, 14, 16

OUT_B, BACK_B, GAIN1, GAIN2, SHIFT1, SHIFT2, IN_B, QKV_B = range(0, 16, 2)


def dot(a, b):
    return jnp.dot(a, b, preferred_element_type=F32)


def dot_nt(a, b):
    return lax.dot_general(a, b, (((1,), (1,)), ((), ())), preferred_element_type=F32)


def dot_tn(a, b):
    return lax.dot_general(a, b, (((0,), (0,)), ((), ())), preferred_element_type=F32)


def nested(structure, flat):
    leaves, tree = jax.tree.flatten(structure)
    return jax.tree.unflatten(tree, flat)


class InHbm:
    def __init__(self, value):
        self.value = value


def run(name, body, meta, ins, outs, limit=6, scratch=(), aliases=None):
    flat_in, flat_out = jax.tree.leaves(ins), jax.tree.leaves(outs)

    def kernel(meta_ref, *refs):
        into = len(flat_in) + len(flat_out)
        body(meta_ref, nested(ins, refs[: len(flat_in)]), nested(outs, refs[len(flat_in) : into]), *refs[into:])

    def spec(leaf):
        return pl.BlockSpec(memory_space=pltpu.HBM if isinstance(leaf, InHbm) else pltpu.VMEM)

    def plain(leaf):
        return leaf.value if isinstance(leaf, InHbm) else leaf

    results = pl.pallas_call(
        kernel,
        name=name,
        in_specs=[pl.BlockSpec(memory_space=pltpu.SMEM)] + [spec(a) for a in flat_in],
        out_specs=[spec(a) for a in flat_out],
        out_shape=[plain(a) for a in flat_out],
        scratch_shapes=list(scratch),
        input_output_aliases={1 + i: o for i, o in (aliases or {}).items()},
        compiler_params=pltpu.CompilerParams(vmem_limit_bytes=limit * MIB),
        cost_estimate=pl.CostEstimate(flops=1, bytes_accessed=1, transcendentals=0),
    )(meta, *[plain(a) for a in flat_in])
    return nested(outs, results)


def arr(shape, dtype=BF16):
    return jax.ShapeDtypeStruct(tuple(shape), dtype)


class Ids:
    def __init__(self, meta, dims):
        self.meta, self.dims = meta, dims
        self.section, self.tensor, self.dp = meta[0], meta[1], meta[2]

    def chain(self, slot):
        return (self.tensor ^ slot) * self.dims.per_chip + self.section

    def kind(self, slot):
        return self.meta[3 + self.chain(slot)]

    def length(self, slot):
        return self.meta[3 + self.dims.group + self.chain(slot)]


def copies(pairs, sems):
    started = [pltpu.make_async_copy(source, target, sems.at[i]) for i, (source, target) in enumerate(pairs)]
    for copy in started:
        copy.start()
    return started


def fetch(dims, layer, meta, own, other, name):
    def body(meta_ref, ins, outs, sems):
        own, other = ins
        ids = Ids(meta_ref, dims)

        def go(source):
            for copy in copies(list(zip(source, outs)), sems):
                copy.wait()

        pl.when(ids.section == layer)(lambda: go(own))
        pl.when(ids.section != layer)(lambda: go(other))

    ins = ([InHbm(w) for w in own], [InHbm(w) for w in other])
    outs = [arr(w.shape, w.dtype) for w in own]
    return run(f"fetch_{name}{layer}", body, meta, ins, outs, scratch=[pltpu.SemaphoreType.DMA((len(own),))])


def pack_weights(dims, meta, qkv_w, out_w):
    rows = qkv_w.shape[1]

    def body(meta_ref, ins, outs, sems):
        pairs = [(ins[0], outs.at[:, :rows]), (ins[1], outs.at[:, rows:])]
        for copy in copies(pairs, sems):
            copy.wait()

    out = InHbm(arr((TYPES, rows + out_w.shape[1], dims.d)))
    ins = (InHbm(qkv_w), InHbm(out_w))
    return run("pack_w", body, meta, ins, out, scratch=[pltpu.SemaphoreType.DMA((2,))])


class Dims:
    pass


def attention_forward(dims, layer, meta, slot, rows, weight, small):
    length, width = dims.length, dims.width

    def body(meta_ref, ins, outs):
        rows, weight, small = ins
        part, qkv, att = outs
        ids = Ids(meta_ref, dims)
        kind = ids.kind(slot)
        bias = small[pl.ds(QKV_B + kind, 1), : 3 * width]
        qkv[...] = (dot_nt(rows[...], weight[kind, : 3 * width, :]) + bias).astype(BF16)
        keep = lax.broadcasted_iota(jnp.int32, (1, length), 1) < ids.length(slot)
        for c in range(0, width, HEAD_DIM):
            query = qkv[:, c : c + HEAD_DIM]
            key = qkv[:, width + c : width + c + HEAD_DIM]
            value = qkv[:, 2 * width + c : 2 * width + c + HEAD_DIM]
            scores = jnp.where(keep, dot_nt(query, key) * SCALE, -1e9)
            expd = jnp.exp(scores - jnp.max(scores, axis=-1, keepdims=True))
            probs = (expd * (1.0 / jnp.sum(expd, axis=-1, keepdims=True))).astype(BF16)
            att[:, c : c + HEAD_DIM] = dot(probs, value).astype(BF16)
        part[...] = dot(att[...], weight[kind, 3 * width :, :]).astype(BF16)

    outs = (arr((length, dims.d)), arr((length, 3 * width)), arr((length, width)))
    return run(f"attn_fwd{layer}_{slot}", body, meta, (rows, weight, small), outs)


def attention_backward(dims, layer, meta, slot, grads, qkv, weight):
    length, width = dims.length, dims.width

    def body(meta_ref, ins, outs):
        grads, qkv, weight = ins
        part, dqkv = outs
        ids = Ids(meta_ref, dims)
        kind = ids.kind(slot)
        keep = lax.broadcasted_iota(jnp.int32, (1, length), 1) < ids.length(slot)
        datt = dot_nt(grads[:length, :], weight[kind, 3 * width :, :]).astype(BF16)
        for c in range(0, width, HEAD_DIM):
            query = qkv[:, c : c + HEAD_DIM]
            key = qkv[:, width + c : width + c + HEAD_DIM]
            value = qkv[:, 2 * width + c : 2 * width + c + HEAD_DIM]
            da = datt[:, c : c + HEAD_DIM]
            scores = jnp.where(keep, dot_nt(query, key) * SCALE, -1e9)
            expd = jnp.exp(scores - jnp.max(scores, axis=-1, keepdims=True))
            probs = expd * (1.0 / jnp.sum(expd, axis=-1, keepdims=True))
            dprobs = dot_nt(da, value)
            dscores = (probs * (dprobs - jnp.sum(probs * dprobs, axis=-1, keepdims=True))).astype(BF16)
            dqkv[:, c : c + HEAD_DIM] = (dot(dscores, key) * SCALE).astype(BF16)
            dqkv[:, width + c : width + c + HEAD_DIM] = (dot_tn(dscores, query) * SCALE).astype(BF16)
            dqkv[:, 2 * width + c : 2 * width + c + HEAD_DIM] = dot_tn(probs.astype(BF16), da).astype(BF16)
        part[...] = dot(dqkv[...], weight[kind, : 3 * width, :]).astype(BF16)

    outs = (arr((length, dims.d)), arr((length, 3 * width)))
    return run(f"attn_bwd{layer}_{slot}", body, meta, (grads, qkv, weight), outs)


def typed_sum(ids, left, right, kind, slots):
    chosen = [
        jnp.where(ids.kind(k) == kind, right[k], jnp.zeros_like(right[k])) for k in range(slots)
    ]
    return dot_tn(jnp.concatenate(left, axis=0), jnp.concatenate(chosen, axis=0))


def halved(value):
    high = value.astype(BF16)
    return high, (value - high.astype(F32)).astype(BF16)


def carried(ids, blocks, slots, r):
    found = []
    for kind in range(TYPES):
        total = jnp.zeros((3, blocks[0].shape[1]), F32)
        for k in range(slots):
            tail = blocks[k][r : r + TAIL, :].astype(F32)
            total = total + jnp.where(ids.kind(k) == kind, tail[0:3] + tail[3:6], 0.0)
        found.append(total)
    return jnp.concatenate(found, axis=0)


def row_sums(ids, slots, rows):
    found = []
    for kind in range(TYPES):
        total = 0.0
        for k in range(slots):
            here = jnp.sum(rows[k].astype(F32), axis=0, keepdims=True)
            total = total + jnp.where(ids.kind(k) == kind, here, 0.0)
        found.append(total)
    return jnp.concatenate(found, axis=0)


def attention_weights(dims, layer, meta, rows, dqkv, grads, att, below):
    length, slots, width, d = dims.length, dims.slots, dims.width, dims.d

    def body(meta_ref, ins, outs):
        rows, dqkv, grads, att, below = ins
        ids = Ids(meta_ref, dims)
        left = [ref[...] for ref in rows]
        back = [ref[:length, :] for ref in grads]
        right = [ref[...] for ref in dqkv]
        heads = [ref[...] for ref in att]
        for kind in range(TYPES):
            span = slice(kind * d, (kind + 1) * d)
            outs[span, : 3 * width] = typed_sum(ids, left, right, kind, slots).astype(BF16)
            outs[span, 3 * width :] = typed_sum(ids, back, heads, kind, slots).astype(BF16)
        qkv_rows = row_sums(ids, slots, right)
        qkv_rows = jnp.concatenate([qkv_rows, jnp.zeros((TYPES, width), F32)], axis=1)
        firsts = carried(ids, grads, slots, length)
        small = jnp.concatenate([firsts, below[:6, :], qkv_rows, below[6:8, :]], axis=0)
        outs[TYPES * d : TYPES * d + SMALL, :], outs[TYPES * d + SMALL :, :] = halved(small)

    out = arr((TYPES * d + 2 * SMALL, d))
    return run(f"attn_dw{layer}", body, meta, (rows, dqkv, grads, att, below), out, 8)


def ffn_weights(dims, layer, meta, rows, dpre, grads, act):
    length, slots, hidden, d = dims.length, dims.slots, dims.hidden, dims.d

    def body(meta_ref, ins, outs):
        rows, dpre, grads, act = ins
        total, small = outs
        ids = Ids(meta_ref, dims)
        for step, (left, right) in enumerate(((rows, dpre), (grads, act))):
            left_rows = [ref[:length, :] for ref in left]
            right_rows = [ref[...] for ref in right]
            for kind in range(TYPES):
                first = (TYPES * step + kind) * d
                total[first : first + d, :] = typed_sum(ids, left_rows, right_rows, kind, slots).astype(BF16)
        small[0:6, :] = carried(ids, grads, slots, length)
        small[6:8, :] = row_sums(ids, slots, [ref[...] for ref in dpre])

    outs = (arr((2 * TYPES * d, hidden)), arr((8, hidden), F32))
    return run(f"ffn_dw{layer}", body, meta, (rows, dpre, grads, act), outs, 8)


def ffn_forward(dims, layer, meta, slot, rows, weight, small):
    length, hidden = dims.length, dims.hidden

    def body(meta_ref, ins, outs):
        rows, (in_w, back_w), small = ins
        part, act, slope = outs
        kind = Ids(meta_ref, dims).kind(slot)
        pre = dot(rows[...], in_w[kind]) + small[pl.ds(IN_B + kind, 1), :hidden]
        gate = 0.5 * (1.0 + lax.erf(pre * HALF_ROOT))
        act[...] = (pre * gate).astype(BF16)
        slope[...] = (gate + pre * (DENSITY * jnp.exp(-0.5 * pre * pre))).astype(BF16)
        part[...] = dot(act[...], back_w[kind]).astype(BF16)

    outs = (arr((length, dims.d)), arr((length, hidden)), arr((length, hidden)))
    return run(f"ffn_fwd{layer}_{slot}", body, meta, (rows, weight, small), outs)


def ffn_backward(dims, layer, meta, slot, grads, slope, weight):
    length, hidden = dims.length, dims.hidden

    def body(meta_ref, ins, outs):
        grads, slope, (in_w, back_w) = ins
        part, dpre = outs
        kind = Ids(meta_ref, dims).kind(slot)
        dact = dot_nt(grads[:length, :], back_w[kind])
        dpre[...] = (dact * slope[...].astype(F32)).astype(BF16)
        part[...] = dot_nt(dpre[...], in_w[kind]).astype(BF16)

    outs = (arr((length, dims.d)), arr((length, hidden)))
    return run(f"ffn_bwd{layer}_{slot}", body, meta, (grads, slope, weight), outs)


def normalized(values):
    center = values - jnp.mean(values, axis=-1, keepdims=True)
    inv = lax.rsqrt(jnp.mean(center * center, axis=-1, keepdims=True) + EPS)
    return center * inv, inv


def summed(parts):
    total = parts[0][...].astype(F32)
    for part in parts[1:]:
        total = total + part[...].astype(F32)
    return total


def norm_back(grad, normal, inv, gain):
    scaled = grad * gain
    return inv * (
        scaled
        - jnp.mean(scaled, axis=-1, keepdims=True)
        - normal * jnp.mean(scaled * normal, axis=-1, keepdims=True)
    )


def with_sums(low, value, sums):
    r = value.shape[0]
    low[:r, :] = value.astype(BF16)
    total = jnp.concatenate([jnp.sum(v, axis=0, keepdims=True) for v in sums], axis=0)
    high, rest = halved(total)
    blank = jnp.zeros((TAIL - 6, value.shape[1]), BF16)
    low[r:, :] = jnp.concatenate([high, rest, blank], axis=0)


def first_norm(dims, layer, meta, own_rows, parts, small):
    r, d = dims.length, dims.d

    def body(meta_ref, ins, outs):
        own_rows, parts, small = ins
        low, normal, inv = outs
        kind = Ids(meta_ref, dims).kind(0)
        mixed = own_rows[...].astype(F32) + summed(parts) + small[pl.ds(OUT_B + kind, 1), :]
        xhat, scale = normalized(mixed)
        normal[...] = xhat
        inv[...] = jnp.broadcast_to(scale, inv.shape)
        low[...] = (xhat * small[pl.ds(GAIN1 + kind, 1), :] + small[pl.ds(SHIFT1 + kind, 1), :]).astype(BF16)

    outs = (arr((r, d)), arr((r, d), F32), arr((r, 128), F32))
    return run(f"norm1_{layer}", body, meta, (own_rows, parts, small), outs)


def second_values(kind, normal, parts, small):
    normed = normal[...] * small[pl.ds(GAIN1 + kind, 1), :] + small[pl.ds(SHIFT1 + kind, 1), :]
    xhat, scale = normalized(normed + summed(parts) + small[pl.ds(BACK_B + kind, 1), :])
    output = xhat * small[pl.ds(GAIN2 + kind, 1), :] + small[pl.ds(SHIFT2 + kind, 1), :]
    return xhat, scale, output.astype(BF16)


def second_norm(dims, layer, meta, normal, parts, small):
    r, d = dims.length, dims.d

    def body(meta_ref, ins, outs):
        normal, parts, small = ins
        low, xhat_ref, inv = outs
        kind = Ids(meta_ref, dims).kind(0)
        xhat, scale, low[...] = second_values(kind, normal, parts, small)
        xhat_ref[...] = xhat
        inv[...] = jnp.broadcast_to(scale, inv.shape)

    outs = (arr((r, d)), arr((r, d), F32), arr((r, 128), F32))
    return run(f"norm2_{layer}", body, meta, (normal, parts, small), outs)


def second_back(kind, grad, xhat, scale, small, second_grad, low):
    value = norm_back(grad, xhat, scale, small[pl.ds(GAIN2 + kind, 1), :])
    second_grad[...] = value
    with_sums(low, value, (grad * xhat, grad, value))


def last_norm(dims, layer, meta, normal, parts, small, cotangent):
    r, d = dims.length, dims.d

    def body(meta_ref, ins, outs):
        normal, parts, small, cotangent = ins
        act, second_grad, low = outs
        ids = Ids(meta_ref, dims)
        kind = ids.kind(0)
        xhat, scale, act[...] = second_values(kind, normal, parts, small)
        grad = cotangent[ids.section].astype(F32)
        second_back(kind, grad, xhat, scale, small, second_grad, low)

    outs = (arr((r, d)), arr((r, d), F32), arr((r + TAIL, d)))
    return run(f"norm2_{layer}", body, meta, (normal, parts, small, cotangent), outs)


def between_layers(dims, layer, meta, parts, first_grad, xhat, inv, small):
    r, d = dims.length, dims.d

    def body(meta_ref, ins, outs):
        parts, first_grad, xhat, inv, small = ins
        input_grad, second_grad, low = outs
        kind = Ids(meta_ref, dims).kind(0)
        value = summed(parts) + first_grad[...]
        input_grad[...] = value
        grad = value.astype(BF16).astype(F32)
        second_back(kind, grad, xhat[...], inv[:, :1], small, second_grad, low)

    outs = (arr((r, d), F32), arr((r, d), F32), arr((r + TAIL, d)))
    return run(f"between{layer}", body, meta, (parts, first_grad, xhat, inv, small), outs)


def first_back(dims, layer, meta, parts, second_grad, xhat, inv, small):
    r, d = dims.length, dims.d

    def body(meta_ref, ins, outs):
        parts, second_grad, xhat, inv, small = ins
        first_grad, low = outs
        kind = Ids(meta_ref, dims).kind(0)
        grad = summed(parts) + second_grad[...]
        value = norm_back(grad, xhat[...], inv[:, :1], small[pl.ds(GAIN1 + kind, 1), :])
        first_grad[...] = value
        with_sums(low, value, (grad * xhat[...], grad, value))

    outs = (arr((r, d), F32), arr((r + TAIL, d)))
    return run(f"norm1_back{layer}", body, meta, (parts, second_grad, xhat, inv, small), outs)


def input_gradient(dims, layer, meta, parts, first_grad):
    def body(meta_ref, ins, outs):
        parts, first_grad = ins
        outs[...] = summed(parts) + first_grad[...]

    return run(f"input_grad{layer}", body, meta, (parts, first_grad), arr((dims.length, dims.d), F32))


def swap(value, axis, bit):
    count = lax.axis_size(axis)
    return lax.ppermute(value, axis, [(source, source ^ bit) for source in range(count)])


def gather(value, slots):
    return [value] + [swap(value, "tensor", k) for k in range(1, slots)]


def scatter(parts):
    return [parts[0]] + [swap(part, "tensor", k) for k, part in enumerate(parts) if k]


def tied(*values):
    return lax.optimization_barrier(values)


class GradSum:
    def __init__(self, dims, layer, meta, name, small):
        self.dims, self.layer, self.meta, self.name = dims, layer, meta, f"{name}{layer}"
        self.small = small

    def start(self, value):
        self.value = value
        self.d, self.cols = self.dims.d, value.shape[1]
        self.count = value.shape[0] // self.d
        self.rows = self.d // self.dims.dp
        self.extra = 2 * SMALL if self.small else 0
        self.other = lax.ppermute(value, "section", [(1 - self.layer, self.layer)])

    def permute(self, value, bit):
        base = self.layer * self.dims.dp
        pairs = [(base + z, base + (z ^ bit)) for z in range(self.dims.dp)]
        return lax.ppermute(value, ("section", "dp"), pairs)

    def whole(self, ref, base):
        return ref[base : base + SMALL, :].astype(F32) + ref[base + SMALL : base + 2 * SMALL, :].astype(F32)

    def near_sum(self):
        dims, rows, count, cols, d = self.dims, self.rows, self.count, self.cols, self.d
        if dims.dp != 4:
            both = self.value.astype(F32) + self.other.astype(F32)
            if self.small:
                low = both[count * d :]
                self.total_small = lax.psum(low[:SMALL] + low[SMALL:], "dp")
            return both[: count * d].reshape(count, d, cols).astype(BF16)
        base = 2 * count * rows

        def body(meta_ref, ins, outs):
            value, other = ins
            sent, kept = outs
            odd = lax.rem(Ids(meta_ref, dims).dp, 2)

            def part(index, chunk):
                start = pl.multiple_of(index * d + chunk * rows, 16)
                return value[pl.ds(start, rows), :].astype(F32) + other[pl.ds(start, rows), :].astype(F32)

            for i in range(2):
                for index in range(count):
                    at = (i * count + index) * rows
                    sent[at : at + rows, :] = part(index, 2 * i + 1 - odd).astype(BF16)
                    kept[at : at + rows, :] = part(index, 2 * i + odd)
            if self.small:
                total = self.whole(value, count * d) + self.whole(other, count * d)
                sent[base : base + SMALL, :], sent[base + SMALL :, :] = halved(total)
                kept[base:, :] = total

        outs = (arr((base + self.extra, cols)), arr((base + self.extra // 2, cols), F32))
        sent, self.kept = run(f"{self.name}_a", body, self.meta, (self.value, self.other), outs)
        return sent

    def near_send(self, sent):
        if self.dims.dp != 4:
            self.pieces = [lax.psum_scatter(sent, "dp", scatter_dimension=1, tiled=True)]
            if self.small:
                self.pieces.append(self.total_small)
        else:
            self.near = self.permute(sent, 1)

    def far_sum(self):
        dims, cols, size = self.dims, self.cols, self.count * self.rows
        if dims.dp != 4:
            return None

        def body(meta_ref, ins, outs):
            kept, near = ins
            sent, final = outs
            mine = lax.div(Ids(meta_ref, dims).dp, 2)

            def half(i):
                span = pl.ds(pl.multiple_of(i * size, 16), size)
                return kept[span, :] + near[span, :].astype(F32)

            sent[:size, :] = half(1 - mine).astype(BF16)
            final[:size, :] = half(mine)
            if self.small:
                total = kept[2 * size :, :] + self.whole(near, 2 * size)
                sent[size : size + SMALL, :], sent[size + SMALL :, :] = halved(total)
                final[size:, :] = total

        outs = (arr((size + self.extra, cols)), arr((size + self.extra // 2, cols), F32))
        sent, self.final = run(f"{self.name}_b", body, self.meta, (self.kept, self.near), outs)
        return sent

    def far_send(self, sent):
        if self.dims.dp == 4:
            self.pieces = [self.final, self.permute(sent, 2)]

    def finish(self, shapes, put, before=None):
        dims, rows, size = self.dims, self.rows, self.count * self.rows
        flat = len(self.pieces)

        def body(meta_ref, ins, outs, *scratch):
            pieces, values, sems = ins[0], scratch[:-1], scratch[-1]

            def total(index):
                if dims.dp != 4:
                    return pieces[0][index].astype(F32)
                span = slice(index * rows, (index + 1) * rows)
                return pieces[0][span, :] + pieces[1][span, :].astype(F32)

            @pl.when(Ids(meta_ref, dims).section == self.layer)
            def _():
                small = None
                if self.small:
                    small = pieces[0][size:, :] + self.whole(pieces[1], size) if dims.dp == 4 else pieces[1][...]
                put(values, [total(index) for index in range(self.count)], small)
                for copy in copies(list(zip(values, outs)), sems):
                    copy.wait()

        outs = [InHbm(arr(shape, F32)) for shape in shapes]
        ins = [self.pieces] + ([] if before is None else [InHbm(a) for a in before])
        aliases = {} if before is None else {flat + i: i for i in range(len(shapes))}
        scratch = [pltpu.VMEM(shape, F32) for shape in shapes] + [pltpu.SemaphoreType.DMA((len(shapes),))]
        return run(f"{self.name}_end", body, self.meta, ins, outs, 8, scratch, aliases)


def pack_params(dims, meta, arrays):
    width = dims.width

    def body(meta_ref, ins, outs, *scratch):
        for copy in copies(list(zip(ins, scratch[:-1])), scratch[-1]):
            copy.wait()
        out_b, back_b, gains, shifts, in_b, qkv_b = scratch[:-1]
        for t in range(TYPES):
            for row, ref in ((OUT_B, out_b), (BACK_B, back_b), (IN_B, in_b)):
                outs[row + t : row + t + 1, :] = ref[0, t : t + 1, :]
            for row, ref in ((GAIN1, gains), (SHIFT1, shifts)):
                for norm in range(2):
                    outs[row + 2 * norm + t : row + 2 * norm + t + 1, :] = ref[0, t, norm : norm + 1, :]
            outs[QKV_B + t : QKV_B + t + 1, :] = jnp.zeros((1, dims.d), F32)
            outs[QKV_B + t : QKV_B + t + 1, :width] = qkv_b[0, t, 0:1, :]
            outs[QKV_B + t : QKV_B + t + 1, 2 * width : 3 * width] = qkv_b[0, t, 1:2, :]

    scratch = [pltpu.VMEM(a.shape, F32) for a in arrays] + [pltpu.SemaphoreType.DMA((len(arrays),))]
    return run("pack", body, meta, [InHbm(a) for a in arrays], arr((16, dims.d), F32), scratch=scratch)


def order_params(dims, meta, own, other):
    def body(meta_ref, ins, outs):
        here = meta_ref[0] == 0
        own, other = ins[0][...], ins[1][...]
        outs[0][...] = jnp.where(here, own, other)
        outs[1][...] = jnp.where(here, other, own)

    return run("params", body, meta, [own, other], [arr(own.shape, F32)] * 2)


def both_chains(dims, meta, own, moved, name):
    def body(meta_ref, ins, outs):
        own, moved = ins
        first = meta_ref[0] == 0

        @pl.when(first)
        def _():
            outs[0, 0] = own[0][...]
            outs[0, 1] = moved[0][...]

        @pl.when(jnp.logical_not(first))
        def _():
            outs[0, 0] = moved[1][...]
            outs[0, 1] = own[1][...]

    return run(name, body, meta, (own, moved), arr((1, 2, dims.length, dims.d), own[0].dtype), 8)


def body(
    tokens,
    cotangent,
    lengths,
    chain_type,
    qkv_weight,
    qkv_bias,
    out_weight,
    out_bias,
    ffn_in,
    ffn_in_bias,
    ffn_out,
    ffn_out_bias,
    norm_gain,
    norm_bias,
):
    dims = Dims()
    dims.per_chip, dims.length, dims.d = tokens.shape
    dims.slots = lax.axis_size("tensor")
    dims.dp = lax.axis_size("dp")
    dims.group = lengths.shape[0]
    dims.width = qkv_weight.shape[-1]
    dims.hidden = ffn_in.shape[-1]
    sections = lax.axis_size("section")
    assert dims.per_chip == sections == LAYERS and dims.slots & (dims.slots - 1) == 0
    assert dims.dp & (dims.dp - 1) == 0 and 4 * dims.width == dims.d == dims.hidden
    d, width, slots = dims.d, dims.width, dims.slots
    each = range(slots)
    section = lax.axis_index("section")
    meta = jnp.concatenate(
        [
            jnp.stack([section, lax.axis_index("tensor"), lax.axis_index("dp")]).astype(jnp.int32),
            chain_type,
            lengths,
        ]
    )

    own_rows = jnp.where(section == 0, tokens[0], tokens[1])
    rows = gather(own_rows, slots)

    qkv_own = qkv_weight[0].transpose(0, 2, 3, 1).reshape(TYPES, 3 * width, d)
    attn_own = pack_weights(dims, meta, qkv_own, out_weight[0])
    attn_other = swap(attn_own, "section", 1)
    packed = pack_params(
        dims, meta, (out_bias, ffn_out_bias, norm_gain, norm_bias, ffn_in_bias, qkv_bias)
    )
    small = order_params(dims, meta, packed, swap(packed, "section", 1))
    ffn_own = [ffn_in[0], ffn_out[0]]

    def moved(value, layer):
        return lax.ppermute(value, "section", [(1 - layer, layer)])

    saved = []
    acts = []
    for layer in range(LAYERS):
        (weight,) = fetch(dims, layer, meta, [attn_own], [attn_other], "attn")
        attn = [attention_forward(dims, layer, meta, k, rows[k], weight, small[layer]) for k in each]
        parts, qkv, att = ([a[i] for a in attn] for i in range(3))
        parts = scatter(parts)
        if layer == 0:
            parts, ffn_sent = tied(parts, ffn_own)
            ffn_other = [swap(w, "section", 1) for w in ffn_sent]
        first = first_norm(dims, layer, meta, own_rows, parts, small[layer])
        normed = gather(first[0], slots)
        weight = fetch(dims, layer, meta, ffn_own, ffn_other, "ffn")
        ffn = [ffn_forward(dims, layer, meta, k, normed[k], weight, small[layer]) for k in each]
        parts, act, slope = ([f[i] for f in ffn] for i in range(3))
        parts = scatter(parts)
        if layer < LAYERS - 1:
            second = second_norm(dims, layer, meta, first[1], parts, small[layer])
        else:
            second = last_norm(dims, layer, meta, first[1], parts, small[layer], cotangent)
        saved.append((rows, qkv, att, first, normed, act, slope, second))
        own_rows = second[0]
        acts.append(own_rows)
        if layer < LAYERS - 1:
            rows = gather(own_rows, slots)

    second_grad, low = second[1:]
    input_grads = [None] * LAYERS
    ffn_sums = [GradSum(dims, layer, meta, "ffn", False) for layer in range(LAYERS)]
    attn_sums = [GradSum(dims, layer, meta, "attn", True) for layer in range(LAYERS)]
    for layer in reversed(range(LAYERS)):
        rows, qkv, att, first, normed, act, slope, second = saved[layer]
        top = layer == LAYERS - 1
        grads = gather(low, slots)
        weight = fetch(dims, layer, meta, ffn_own, ffn_other, "ffn_back")
        if top:
            acts_moved = [moved(acts[i], i) for i in range(LAYERS)]
        else:
            near = attn_sums[layer + 1].near_sum()
            far = ffn_sums[layer + 1].far_sum()
            grads, near, far = tied(grads, near, far)
            attn_sums[layer + 1].near_send(near)
            ffn_sums[layer + 1].far_send(far)
        back = [ffn_backward(dims, layer, meta, k, grads[k], slope[k], weight) for k in each]
        parts, dpre = ([b[i] for b in back] for i in range(2))
        parts = scatter(parts)
        ffn_grad, below = ffn_weights(dims, layer, meta, normed, dpre, grads, act)
        if top:
            acts_out = both_chains(dims, meta, acts, acts_moved, "acts_out")
            parts, ffn_grad, acts_out = tied(parts, ffn_grad, acts_out)
        else:
            parts, ffn_grad = tied(parts, ffn_grad)
        ffn_sums[layer].start(ffn_grad)
        first_grad, low = first_back(
            dims, layer, meta, parts, second_grad, first[1], first[2], small[layer]
        )
        grads = gather(low, slots)
        (weight,) = fetch(dims, layer, meta, [attn_own], [attn_other], "attn_back")
        near = ffn_sums[layer].near_sum()
        if top:
            grads, near = tied(grads, near)
        else:
            far = attn_sums[layer + 1].far_sum()
            grads, near, far = tied(grads, near, far)
            attn_sums[layer + 1].far_send(far)
        ffn_sums[layer].near_send(near)
        back = [attention_backward(dims, layer, meta, k, grads[k], qkv[k], weight) for k in each]
        parts, dqkv = ([b[i] for b in back] for i in range(2))
        parts = scatter(parts)
        attn_grad = attention_weights(dims, layer, meta, rows, dqkv, grads, att, below)
        parts, attn_grad = tied(parts, attn_grad)
        attn_sums[layer].start(attn_grad)
        if layer > 0:
            second = saved[layer - 1][-1]
            input_grads[layer], second_grad, low = between_layers(
                dims, layer, meta, parts, first_grad, second[1], second[2], small[layer - 1]
            )
        else:
            input_grads[layer] = input_gradient(dims, layer, meta, parts, first_grad)

    share = d // dims.dp
    ffn_shapes = [(TYPES, share, dims.hidden)] * 2
    attn_shapes = [
        (TYPES, 3, share, width),
        (TYPES, width, share),
        (1, TYPES, 2, width),
        (1, TYPES, d),
        (1, TYPES, dims.hidden),
        (1, TYPES, d),
        (1, TYPES, 2, d),
        (1, TYPES, 2, d),
    ]

    def put_ffn(outs, totals, small):
        for index, total in enumerate(totals):
            outs[index // TYPES][index % TYPES] = total

    def put_attn(outs, totals, small):
        qkv_out, out_out, qkv_b, out_b, in_b, back_b, gains, shifts = outs
        for kind, total in enumerate(totals):
            for i in range(3):
                qkv_out[kind, i] = total[:, i * width : (i + 1) * width]
            out_out[kind] = total[:, 3 * width :].T
            qkv_b[0, kind, 0:1, :] = small[QKV_SUMS + kind : QKV_SUMS + kind + 1, :width]
            qkv_b[0, kind, 1:2, :] = small[QKV_SUMS + kind : QKV_SUMS + kind + 1, 2 * width : 3 * width]
            in_b[0, kind : kind + 1, :] = small[IN_SUMS + kind : IN_SUMS + kind + 1, :]
            for norm, (base, bias) in enumerate(((FIRST_SUMS, out_b), (SECOND_SUMS, back_b))):
                row = base + 3 * kind
                gains[0, kind, norm : norm + 1, :] = small[row : row + 1, :]
                shifts[0, kind, norm : norm + 1, :] = small[row + 1 : row + 2, :]
                bias[0, kind : kind + 1, :] = small[row + 2 : row + 3, :]

    ffn_out_grads = ffn_sums[1].finish(ffn_shapes, put_ffn)
    attn_out_grads = attn_sums[1].finish(attn_shapes, put_attn)
    near, far = tied(attn_sums[0].near_sum(), ffn_sums[0].far_sum())
    attn_sums[0].near_send(near)
    ffn_sums[0].far_send(far)
    attn_sums[0].far_send(attn_sums[0].far_sum())

    grads_moved = [moved(input_grads[layer], layer) for layer in range(LAYERS)]
    grads_out = both_chains(dims, meta, input_grads, grads_moved, "grads_out")
    in_total, back_total = ffn_sums[0].finish(ffn_shapes, put_ffn, ffn_out_grads)
    qkv_total, out_total, *small_grads = attn_sums[0].finish(attn_shapes, put_attn, attn_out_grads)
    qkv_bias_out, out_bias_out, in_bias_out, back_bias_out, gain_out, shift_out = small_grads
    return (
        acts_out,
        grads_out,
        qkv_total.transpose(0, 2, 1, 3)[None],
        qkv_bias_out,
        out_total[None],
        out_bias_out,
        in_total[None],
        in_bias_out,
        back_total.transpose(0, 2, 1)[None],
        back_bias_out,
        gain_out,
        shift_out,
    )


def solution(mesh):
    placed = (
        P(("dp", "tensor"), None, None),
        P(("dp", "tensor"), None, None),
        P("dp"),
        P("dp"),
        P("section", None, None, None, "tensor"),
        P("section", None, None, "tensor"),
        P("section", None, "tensor", None),
        P("section", None, None),
        P("section", None, None, "tensor"),
        P("section", None, "tensor"),
        P("section", None, "tensor", None),
        P("section", None, None),
        P("section", None, None, None),
        P("section", None, None, None),
    )
    return jax.shard_map(
        body,
        mesh=mesh,
        in_specs=placed,
        out_specs=(
            P("section", ("dp", "tensor"), None, None),
            P("section", ("dp", "tensor"), None, None),
            P("section", None, "dp", None, "tensor"),
            P("section", None, None, "tensor"),
            P("section", None, "tensor", "dp"),
            P("section", None, None),
            P("section", None, "dp", "tensor"),
            P("section", None, "tensor"),
            P("section", None, "tensor", "dp"),
            P("section", None, None),
            P("section", None, None, None),
            P("section", None, None, None),
        ),
        check_vma=False,
    )
```

time: 494 us -> 366 us (0.74); the launches traced: 485 us -> 363 us
  waiting for transfers between devices: 243 us -> 144 us
  local copies, waits for them, and re-layouts: 42.5 us -> 3.34 us
  Pallas kernels: 93.3 us -> 125 us
  starting transfers between devices: 97.8 us -> 88.9 us
  other arithmetic: 6.51 us -> 0.03 us
    ppermute x63 -> x52, waiting for transfers between devices: 194 us -> 53.2 us  [swap(): lax.ppermute(value, axis, [(source, source ^ bit) for source in range(cou...]
    pallas_call x33 -> x69, Pallas kernels: 93.3 us -> 125 us  [run(): pl.pallas_call(kernel, name=name, in_specs=[pl.BlockSpec(memory_space=plt...]
    ppermute x8, waiting for transfers between devices: 48.9 us -> 74.4 us  [permute(): return lax.ppermute(value, ('section', 'dp'), pairs)]
    unnamed x86 -> x24, local copies, waits for them, and re-layouts: 26.3 us -> 2.6 us
    ppermute x4 -> x8, waiting for transfers between devices: 0.01 us -> 16.7 us  [the longest x4 15.4 us: start(): self.other = lax.ppermute(value, 'section', [(1 - self.layer, self.layer)])]
    ppermute x63 -> x52, starting transfers between devices: 74.9 us -> 61.3 us  [swap(): lax.ppermute(value, axis, [(source, source ^ bit) for source in range(cou...]
    ppermute x4 -> x8, starting transfers between devices: 5.78 us -> 12.6 us  [the longest x4 6.96 us: moved(): return lax.ppermute(value, 'section', [(1 - layer, layer)])]
  transfers between devices with their start and end apart: 75 -> 68, of which waited for: 45 -> 25; matrix products, arithmetic and copies ran while one was open for 5% -> 0% of each run, Pallas kernels for 11% -> 30%
where the time goes in v2:
time: 366 us; the launch traced here: 363 us
  waiting for transfers between devices  144 us (39%)
  Pallas kernels  125 us (34%)
  starting transfers between devices  88.9 us (24%)
    pallas_call x69, Pallas kernels, run(): pl.pallas_call(kernel, name=name, in_specs=[pl.BlockSpec(memory_space=plt...  125 us
    ppermute x8, waiting for transfers between devices, permute(): return lax.ppermute(value, ('section', 'dp'), pairs)  74.4 us
    ppermute x52, starting transfers between devices, swap(): lax.ppermute(value, axis, [(source, source ^ bit) for source in range(cou...  61.3 us
    ppermute x52, waiting for transfers between devices, swap(): lax.ppermute(value, axis, [(source, source ^ bit) for source in range(cou...  53.2 us
    ppermute x4, waiting for transfers between devices, start(): self.other = lax.ppermute(value, 'section', [(1 - self.layer, self.layer)])  15.4 us
    ppermute x8, starting transfers between devices, permute(): return lax.ppermute(value, ('section', 'dp'), pairs)  15 us
  transfers between devices with their start and end apart: 68, of which 25 were waited for; matrix products, arithmetic and copies ran while one was open for 0% of the time, Pallas kernels for 30%

profile of v2, /device:TPU:0, one launch (start us, length us, event | category | flops | bytes accessed | tf_op | source)
XLA Modules:
  0.0 363.1 jit_solution(7321951549719837646)
XLA Ops:
  5.4 3.5 collective-permute-start.6
  12.9 2.9 collective-permute-done.6.refs_0_.refs_3_
  18.0 2.9 collective-permute-start.7
  31.7 2.9 collective-permute-done.3.refs_2_
  39.6 2.9 collective-permute-done.9.refs_3_
  57.2 3.6 collective-permute-done.13.refs_3_
  66.1 12.9 %fetch_attn1.1.refs_1_ = bf16[2,768,768]{2,1,0:T(8,128)(2,1)S(1)} custom-call(s32[19]{0:T(128)S(1)} %concatenate.3.meta_ref, bf16[2,768,768]{2,1,0:T(8,128)(2,1)S(1)} %pack_w.1.refs_0_, bf16[2,768,768]{2,1,0:T(8,128)(2,1)} %collective-permute-done.refs_1_), custom_call_target="tpu_custom_call" | custom-call | flops 1 | bytes 1 | tf_op jit(solution)/shard_map/fetch_attn1/pallas_call | solution.py:64
  91.4 5.2 %collective-permute-done.19.refs_3_ = bf16[160,768]{1,0:T(8,128)(2,1)S(1)} collective-permute-done((bf16[160,768]{1,0:T(8,128)(2,1)S(1)}, bf16[160,768]{1,0:T(8,128)(2,1)S(1)}, u32[]{:S(2)}, u32[]{:S(2)}) %collective-permute-start.19) | collective-permute-done | bytes 245792 | tf_op jit(solution)/shard_map/ppermute | solution.py:436
  101.9 4.1 %collective-permute-done.22.refs_0_.refs_1_ = bf16[160,768]{1,0:T(8,128)(2,1)S(1)} collective-permute-done((bf16[160,768]{1,0:T(8,128)(2,1)S(1)}, bf16[160,768]{1,0:T(8,128)(2,1)S(1)}, u32[]{:S(2)}, u32[]{:S(2)}) %collective-permute-start.22) | collective-permute-done | bytes 245792 | tf_op jit(solution)/shard_map/ppermute | solution.py:436
  115.7 4.8 %collective-permute-done.27.refs_4_ = bf16[160,768]{1,0:T(8,128)(2,1)S(1)} collective-permute-done((bf16[160,768]{1,0:T(8,128)(2,1)S(1)}, bf16[160,768]{1,0:T(8,128)(2,1)S(1)}, u32[]{:S(2)}, u32[]{:S(2)}) %collective-permute-start.27) | collective-permute-done | bytes 245792 | tf_op jit(solution)/shard_map/ppermute | solution.py:436
  127.5 3.1 collective-permute-start.35
  141.6 4.5 %ffn_dw1.1 = (bf16[3072,768]{1,0:T(8,128)(2,1)S(1)}, f32[8,768]{1,0:T(8,128)S(1)}) custom-call(s32[19]{0:T(128)S(1)} %concatenate.3.meta_ref, bf16[160,768]{1,0:T(8,128)(2,1)S(1)} %get-tuple-element.233.refs_0_, bf16[160,768]{1,0:T(8,128)(2,1)S(1)} %collective-permute-done.22.refs_0_.refs_1_, bf16[160,768]{1,0:T(8,128)(2,1)S(1)} %collective-permute-done.24.refs_0_.refs_2_, ...), custom_call_target="tpu_custom_call" | custom-call | flops 1 | bytes 1 | tf_op jit(solution)/shard_map/ffn_dw1/pallas_call | solution.py:64
  159.2 3.8 %collective-permute-done.37.refs_0_.refs_10_ = bf16[176,768]{1,0:T(8,128)(2,1)S(1)} collective-permute-done((bf16[176,768]{1,0:T(8,128)(2,1)S(1)}, bf16[176,768]{1,0:T(8,128)(2,1)S(1)}, u32[]{:S(2)}, u32[]{:S(2)}) %collective-permute-start.37) | collective-permute-done | bytes 270368 | tf_op jit(solution)/shard_map/ppermute | solution.py:436
  163.0 2.8 attn_bwd1_2.1
  166.8 2.8 attn_bwd1_3.1
  171.4 2.8 attn_bwd1_1.1
  175.1 2.8 attn_bwd1_0.1
  177.9 3.2 attn_dw1.1.refs_0_
  193.3 3.4 collective-permute-done.45.refs_0_.refs_11_
  196.7 5.4 %collective-permute-done.44.refs_0_.refs_10_ = bf16[176,768]{1,0:T(8,128)(2,1)S(1)} collective-permute-done((bf16[176,768]{1,0:T(8,128)(2,1)S(1)}, bf16[176,768]{1,0:T(8,128)(2,1)S(1)}, u32[]{:S(2)}, u32[]{:S(2)}) %collective-permute-start.44) | collective-permute-done | bytes 270368 | tf_op jit(solution)/shard_map/ppermute | solution.py:436
  211.7 4.5 %ffn_dw0.1 = (bf16[3072,768]{1,0:T(8,128)(2,1)S(1)}, f32[8,768]{1,0:T(8,128)S(1)}) custom-call(s32[19]{0:T(128)S(1)} %concatenate.3.meta_ref, bf16[160,768]{1,0:T(8,128)(2,1)S(1)} %get-tuple-element.217.refs_0_, bf16[160,768]{1,0:T(8,128)(2,1)S(1)} %collective-permute-done.10.refs_0_.refs_1_, bf16[160,768]{1,0:T(8,128)(2,1)S(1)} %collective-permute-done.12.refs_0_.refs_2_, ...), custom_call_target="tpu_custom_call" | custom-call | flops 1 | bytes 1 | tf_op jit(solution)/shard_map/ffn_dw0/pallas_call | solution.py:64
  224.6 15.2 %collective-permute-done.54.refs_1_ = bf16[3072,768]{1,0:T(8,128)(2,1)S(1)} collective-permute-done((bf16[3072,768]{1,0:T(8,128)(2,1)S(1)}, bf16[3072,768]{1,0:T(8,128)(2,1)S(1)}, u32[]{:S(2)}, u32[]{:S(2)}) %collective-permute-start.54) | collective-permute-done | bytes 4718624 | tf_op jit(solution)/shard_map/ppermute | solution.py:462
  241.3 2.8 attn_bwd0_2.1
  245.5 2.8 attn_bwd0_3.1
  248.9 2.8 attn_bwd0_1.1
  256.2 3.2 attn_dw0.1.refs_0_
  260.8 3.5 collective-permute-start.62
  264.3 37.3 %collective-permute-done.62.refs_1_ = bf16[1536,768]{1,0:T(8,128)(2,1)S(1)} collective-permute-done((bf16[1536,768]{1,0:T(8,128)(2,1)S(1)}, bf16[1536,768]{1,0:T(8,128)(2,1)S(1)}, u32[]{:S(2)}, u32[]{:S(2)}) %collective-permute-start.62) | collective-permute-done | bytes 2359328 | tf_op jit(solution)/shard_map/ppermute | solution.py:467
  306.4 4.5 %collective-permute-start.66 = (bf16[768,768]{1,0:T(8,128)(2,1)S(1)}, bf16[768,768]{1,0:T(8,128)(2,1)S(1)}, u32[]{:S(2)}, u32[]{:S(2)}) collective-permute-start(bf16[768,768]{1,0:T(8,128)(2,1)S(1)} %get-tuple-element.391), channel_id=1, source_target_pairs={{0,8},{4,12},{8,0},{12,4},{1,9},{5,13},{9,1},{13,5},{2,10},{6,14},... | collective-permute-start | bytes 3538952 | tf_op jit(solution)/shard_map/ppermute | solution.py:467
  311.6 23.9 %collective-permute-done.63.refs_1_ = bf16[800,768]{1,0:T(8,128)(2,1)S(1)} collective-permute-done((bf16[800,768]{1,0:T(8,128)(2,1)S(1)}, bf16[800,768]{1,0:T(8,128)(2,1)S(1)}, u32[]{:S(2)}, u32[]{:S(2)}) %collective-permute-start.63) | collective-permute-done | bytes 1228832 | tf_op jit(solution)/shard_map/ppermute | solution.py:467
  345.6 8.4 %collective-permute-done.66.refs_1_ = bf16[768,768]{1,0:T(8,128)(2,1)S(1)} collective-permute-done((bf16[768,768]{1,0:T(8,128)(2,1)S(1)}, bf16[768,768]{1,0:T(8,128)(2,1)S(1)}, u32[]{:S(2)}, u32[]{:S(2)}) %collective-permute-start.66) | collective-permute-done | bytes 1179680 | tf_op jit(solution)/shard_map/ppermute | solution.py:467
  356.1 4.8 %collective-permute-done.64.refs_1_ = bf16[416,768]{1,0:T(8,128)(2,1)S(1)} collective-permute-done((bf16[416,768]{1,0:T(8,128)(2,1)S(1)}, bf16[416,768]{1,0:T(8,128)(2,1)S(1)}, u32[]{:S(2)}, u32[]{:S(2)}) %collective-permute-start.64) | collective-permute-done | bytes 639008 | tf_op jit(solution)/shard_map/ppermute | solution.py:467
  (199 shorter events, 167.3 us)
Async XLA Ops:
  9.0 11.9 %collective-permute-start.4 = (bf16[160,768]{1,0:T(8,128)(2,1)S(1)}, bf16[160,768]{1,0:T(8,128)(2,1)S(1)}, u32[]{:S(2)}, u32[]{:S(2)}) collective-permute-start(bf16[160,768]{1,0:T(8,128)(2,1)S(1)} %select_bitcast_fusion.refs_0_), channel_id=1, source_target_pairs={{0,2},{1,3},{2,0},{3,1},{4,6},{5,7},{6,4},{7,5},{8,10},{9,11},{10,... | collective-permute-start | bytes 737288 | tf_op jit(solution)/shard_map/ppermute | solution.py:436
  9.5 15.3 %collective-permute-start.2 = (bf16[160,768]{1,0:T(8,128)(2,1)S(1)}, bf16[160,768]{1,0:T(8,128)(2,1)S(1)}, u32[]{:S(2)}, u32[]{:S(2)}) collective-permute-start(bf16[160,768]{1,0:T(8,128)(2,1)S(1)} %select_bitcast_fusion.refs_0_), channel_id=1, source_target_pairs={{0,1},{1,0},{2,3},{3,2},{4,5},{5,4},{6,7},{7,6},{8,9},{9,8},{10,11... | collective-permute-start | bytes 737288 | tf_op jit(solution)/shard_map/ppermute | solution.py:436
  18.0 11.8 %collective-permute-start.7 = (bf16[160,768]{1,0:T(8,128)(2,1)S(1)}, bf16[160,768]{1,0:T(8,128)(2,1)S(1)}, u32[]{:S(2)}, u32[]{:S(2)}) collective-permute-start(bf16[160,768]{1,0:T(8,128)(2,1)S(1)} %get-tuple-element.211), channel_id=1, source_target_pairs={{0,3},{1,2},{2,1},{3,0},{4,7},{5,6},{6,5},{7,4},{8,11},{9,10},{10,... | collective-permute-start | bytes 737288 | tf_op jit(solution)/shard_map/ppermute | solution.py:436
  37.5 13.5 %collective-permute-start.12 = (bf16[160,768]{1,0:T(8,128)(2,1)S(1)}, bf16[160,768]{1,0:T(8,128)(2,1)S(1)}, u32[]{:S(2)}, u32[]{:S(2)}) collective-permute-start(bf16[160,768]{1,0:T(8,128)(2,1)S(1)} %get-tuple-element.217.refs_0_), channel_id=1, source_target_pairs={{0,2},{1,3},{2,0},{3,1},{4,6},{5,7},{6,4},{7,5},{8,10},{9,11},{10,... | collective-permute-start | bytes 737288 | tf_op jit(solution)/shard_map/ppermute | solution.py:436
  37.9 14.9 %collective-permute-start.10 = (bf16[160,768]{1,0:T(8,128)(2,1)S(1)}, bf16[160,768]{1,0:T(8,128)(2,1)S(1)}, u32[]{:S(2)}, u32[]{:S(2)}) collective-permute-start(bf16[160,768]{1,0:T(8,128)(2,1)S(1)} %get-tuple-element.217.refs_0_), channel_id=1, source_target_pairs={{0,1},{1,0},{2,3},{3,2},{4,5},{5,4},{6,7},{7,6},{8,9},{9,8},{10,11... | collective-permute-start | bytes 737288 | tf_op jit(solution)/shard_map/ppermute | solution.py:436
  62.6 16.5 %collective-permute-start.16 = (bf16[160,768]{1,0:T(8,128)(2,1)S(1)}, bf16[160,768]{1,0:T(8,128)(2,1)S(1)}, u32[]{:S(2)}, u32[]{:S(2)}) collective-permute-start(bf16[160,768]{1,0:T(8,128)(2,1)S(1)} %get-tuple-element.226.refs_0_), channel_id=1, source_target_pairs={{0,1},{1,0},{2,3},{3,2},{4,5},{5,4},{6,7},{7,6},{8,9},{9,8},{10,11... | collective-permute-start | bytes 737288 | tf_op jit(solution)/shard_map/ppermute | solution.py:436
  64.3 18.7 %collective-permute-start.18 = (bf16[160,768]{1,0:T(8,128)(2,1)S(1)}, bf16[160,768]{1,0:T(8,128)(2,1)S(1)}, u32[]{:S(2)}, u32[]{:S(2)}) collective-permute-start(bf16[160,768]{1,0:T(8,128)(2,1)S(1)} %get-tuple-element.226.refs_0_), channel_id=1, source_target_pairs={{0,2},{1,3},{2,0},{3,1},{4,6},{5,7},{6,4},{7,5},{8,10},{9,11},{10,... | collective-permute-start | bytes 737288 | tf_op jit(solution)/shard_map/ppermute | solution.py:436
  64.7 20.9 %collective-permute-start.20 = (bf16[160,768]{1,0:T(8,128)(2,1)S(1)}, bf16[160,768]{1,0:T(8,128)(2,1)S(1)}, u32[]{:S(2)}, u32[]{:S(2)}) collective-permute-start(bf16[160,768]{1,0:T(8,128)(2,1)S(1)} %get-tuple-element.226.refs_0_), channel_id=1, source_target_pairs={{0,3},{1,2},{2,1},{3,0},{4,7},{5,6},{6,5},{7,4},{8,11},{9,10},{10,... | collective-permute-start | bytes 737288 | tf_op jit(solution)/shard_map/ppermute | solution.py:436
  85.1 11.5 %collective-permute-start.19 = (bf16[160,768]{1,0:T(8,128)(2,1)S(1)}, bf16[160,768]{1,0:T(8,128)(2,1)S(1)}, u32[]{:S(2)}, u32[]{:S(2)}) collective-permute-start(bf16[160,768]{1,0:T(8,128)(2,1)S(1)} %get-tuple-element.230), channel_id=1, source_target_pairs={{0,2},{1,3},{2,0},{3,1},{4,6},{5,7},{6,4},{7,5},{8,10},{9,11},{10,... | collective-permute-start | bytes 737288 | tf_op jit(solution)/shard_map/ppermute | solution.py:436
  99.6 11.3 %collective-permute-start.26 = (bf16[160,768]{1,0:T(8,128)(2,1)S(1)}, bf16[160,768]{1,0:T(8,128)(2,1)S(1)}, u32[]{:S(2)}, u32[]{:S(2)}) collective-permute-start(bf16[160,768]{1,0:T(8,128)(2,1)S(1)} %get-tuple-element.233.refs_0_), channel_id=1, source_target_pairs={{0,3},{1,2},{2,1},{3,0},{4,7},{5,6},{6,5},{7,4},{8,11},{9,10},{10,... | collective-permute-start | bytes 737288 | tf_op jit(solution)/shard_map/ppermute | solution.py:436
  124.9 11.9 %collective-permute-start.28 = (bf16[176,768]{1,0:T(8,128)(2,1)S(1)}, bf16[176,768]{1,0:T(8,128)(2,1)S(1)}, u32[]{:S(2)}, u32[]{:S(2)}) collective-permute-start(bf16[176,768]{1,0:T(8,128)(2,1)S(1)} %get-tuple-element.240.refs_0_.refs_8_), channel_id=1, source_target_pairs={{0,1},{1,0},{2,3},{3,2},{4,5},{5,4},{6,7},{7,6},{8,9},{9,8},{10,11... | collective-permute-start | bytes 811016 | tf_op jit(solution)/shard_map/ppermute | solution.py:436
  126.2 14.1 %collective-permute-start.34 = (bf16[160,768]{1,0:T(8,128)(2,1)S(1)}, bf16[160,768]{1,0:T(8,128)(2,1)S(1)}, u32[]{:S(2)}, u32[]{:S(2)}) collective-permute-start(bf16[160,768]{1,0:T(8,128)(2,1)S(1)} %get-tuple-element.226.refs_0_), channel_id=1, source_target_pairs={{16,0},{17,1},{18,2},{19,3},{20,4},{21,5},{22,6},{23,7},{24,8},{25... | collective-permute-start | bytes 737288 | tf_op jit(solution)/shard_map/ppermute | solution.py:670
  127.5 12.8 %collective-permute-start.35 = (bf16[160,768]{1,0:T(8,128)(2,1)S(1)}, bf16[160,768]{1,0:T(8,128)(2,1)S(1)}, u32[]{:S(2)}, u32[]{:S(2)}) collective-permute-start(bf16[160,768]{1,0:T(8,128)(2,1)S(1)} %get-tuple-element.260.refs_1_), channel_id=1, source_target_pairs={{0,16},{1,17},{2,18},{3,19},{4,20},{5,21},{6,22},{7,23},{8,24},{9,... | collective-permute-start | bytes 737288 | tf_op jit(solution)/shard_map/ppermute | solution.py:670
  132.1 14.1 %collective-permute-start.33 = (bf16[160,768]{1,0:T(8,128)(2,1)S(1)}, bf16[160,768]{1,0:T(8,128)(2,1)S(1)}, u32[]{:S(2)}, u32[]{:S(2)}) collective-permute-start(bf16[160,768]{1,0:T(8,128)(2,1)S(1)} %get-tuple-element.250), channel_id=1, source_target_pairs={{0,3},{1,2},{2,1},{3,0},{4,7},{5,6},{6,5},{7,4},{8,11},{9,10},{10,... | collective-permute-start | bytes 737288 | tf_op jit(solution)/shard_map/ppermute | solution.py:436
  150.8 12.2 %collective-permute-start.37 = (bf16[176,768]{1,0:T(8,128)(2,1)S(1)}, bf16[176,768]{1,0:T(8,128)(2,1)S(1)}, u32[]{:S(2)}, u32[]{:S(2)}) collective-permute-start(bf16[176,768]{1,0:T(8,128)(2,1)S(1)} %get-tuple-element.271.refs_0_.refs_8_), channel_id=1, source_target_pairs={{0,2},{1,3},{2,0},{3,1},{4,6},{5,7},{6,4},{7,5},{8,10},{9,11},{10,... | collective-permute-start | bytes 811016 | tf_op jit(solution)/shard_map/ppermute | solution.py:436
  165.8 15.3 %collective-permute-start.41 = (bf16[160,768]{1,0:T(8,128)(2,1)S(1)}, bf16[160,768]{1,0:T(8,128)(2,1)S(1)}, u32[]{:S(2)}, u32[]{:S(2)}) collective-permute-start(bf16[160,768]{1,0:T(8,128)(2,1)S(1)} %get-tuple-element.279), channel_id=1, source_target_pairs={{0,2},{1,3},{2,0},{3,1},{4,6},{5,7},{6,4},{7,5},{8,10},{9,11},{10,... | collective-permute-start | bytes 737288 | tf_op jit(solution)/shard_map/ppermute | solution.py:436
  169.6 11.5 %collective-permute-start.42 = (bf16[160,768]{1,0:T(8,128)(2,1)S(1)}, bf16[160,768]{1,0:T(8,128)(2,1)S(1)}, u32[]{:S(2)}, u32[]{:S(2)}) collective-permute-start(bf16[160,768]{1,0:T(8,128)(2,1)S(1)} %get-tuple-element.282), channel_id=1, source_target_pairs={{0,3},{1,2},{2,1},{3,0},{4,7},{5,6},{6,5},{7,4},{8,11},{9,10},{10,... | collective-permute-start | bytes 737288 | tf_op jit(solution)/shard_map/ppermute | solution.py:436
  188.0 14.1 %collective-permute-start.44 = (bf16[176,768]{1,0:T(8,128)(2,1)S(1)}, bf16[176,768]{1,0:T(8,128)(2,1)S(1)}, u32[]{:S(2)}, u32[]{:S(2)}) collective-permute-start(bf16[176,768]{1,0:T(8,128)(2,1)S(1)} %get-tuple-element.305.refs_0_.refs_8_), channel_id=1, source_target_pairs={{0,2},{1,3},{2,0},{3,1},{4,6},{5,7},{6,4},{7,5},{8,10},{9,11},{10,... | collective-permute-start | bytes 811016 | tf_op jit(solution)/shard_map/ppermute | solution.py:436
  188.7 13.4 %collective-permute-start.43 = (bf16[176,768]{1,0:T(8,128)(2,1)S(1)}, bf16[176,768]{1,0:T(8,128)(2,1)S(1)}, u32[]{:S(2)}, u32[]{:S(2)}) collective-permute-start(bf16[176,768]{1,0:T(8,128)(2,1)S(1)} %get-tuple-element.305.refs_0_.refs_8_), channel_id=1, source_target_pairs={{0,1},{1,0},{2,3},{3,2},{4,5},{5,4},{6,7},{7,6},{8,9},{9,8},{10,11... | collective-permute-start | bytes 811016 | tf_op jit(solution)/shard_map/ppermute | solution.py:436
  203.6 12.7 %collective-permute-start.49 = (bf16[160,768]{1,0:T(8,128)(2,1)S(1)}, bf16[160,768]{1,0:T(8,128)(2,1)S(1)}, u32[]{:S(2)}, u32[]{:S(2)}) collective-permute-start(bf16[160,768]{1,0:T(8,128)(2,1)S(1)} %get-tuple-element.315), channel_id=1, source_target_pairs={{0,2},{1,3},{2,0},{3,1},{4,6},{5,7},{6,4},{7,5},{8,10},{9,11},{10,... | collective-permute-start | bytes 737288 | tf_op jit(solution)/shard_map/ppermute | solution.py:436
  216.3 23.5 %collective-permute-start.54 = (bf16[3072,768]{1,0:T(8,128)(2,1)S(1)}, bf16[3072,768]{1,0:T(8,128)(2,1)S(1)}, u32[]{:S(2)}, u32[]{:S(2)}) collective-permute-start(bf16[3072,768]{1,0:T(8,128)(2,1)S(1)} %get-tuple-element.335.refs_0_), channel_id=1, source_target_pairs={{16,0},{17,1},{18,2},{19,3},{20,4},{21,5},{22,6},{23,7},{24,8},{25... | collective-permute-start | bytes 14155784 | tf_op jit(solution)/shard_map/ppermute | solution.py:462
  219.3 22.0 %collective-permute-start.53 = (bf16[176,768]{1,0:T(8,128)(2,1)S(1)}, bf16[176,768]{1,0:T(8,128)(2,1)S(1)}, u32[]{:S(2)}, u32[]{:S(2)}) collective-permute-start(bf16[176,768]{1,0:T(8,128)(2,1)S(1)} %get-tuple-element.340.refs_0_.refs_8_), channel_id=1, source_target_pairs={{0,3},{1,2},{2,1},{3,0},{4,7},{5,6},{6,5},{7,4},{8,11},{9,10},{10,... | collective-permute-start | bytes 811016 | tf_op jit(solution)/shard_map/ppermute | solution.py:436
  221.1 20.2 %collective-permute-start.52 = (bf16[176,768]{1,0:T(8,128)(2,1)S(1)}, bf16[176,768]{1,0:T(8,128)(2,1)S(1)}, u32[]{:S(2)}, u32[]{:S(2)}) collective-permute-start(bf16[176,768]{1,0:T(8,128)(2,1)S(1)} %get-tuple-element.340.refs_0_.refs_8_), channel_id=1, source_target_pairs={{0,2},{1,3},{2,0},{3,1},{4,6},{5,7},{6,4},{7,5},{8,10},{9,11},{10,... | collective-permute-start | bytes 811016 | tf_op jit(solution)/shard_map/ppermute | solution.py:436
  222.1 19.3 %collective-permute-start.51 = (bf16[176,768]{1,0:T(8,128)(2,1)S(1)}, bf16[176,768]{1,0:T(8,128)(2,1)S(1)}, u32[]{:S(2)}, u32[]{:S(2)}) collective-permute-start(bf16[176,768]{1,0:T(8,128)(2,1)S(1)} %get-tuple-element.340.refs_0_.refs_8_), channel_id=1, source_target_pairs={{0,1},{1,0},{2,3},{3,2},{4,5},{5,4},{6,7},{7,6},{8,9},{9,8},{10,11... | collective-permute-start | bytes 811016 | tf_op jit(solution)/shard_map/ppermute | solution.py:436
  244.2 15.3 %collective-permute-start.57 = (bf16[160,768]{1,0:T(8,128)(2,1)S(1)}, bf16[160,768]{1,0:T(8,128)(2,1)S(1)}, u32[]{:S(2)}, u32[]{:S(2)}) collective-permute-start(bf16[160,768]{1,0:T(8,128)(2,1)S(1)} %get-tuple-element.348), channel_id=1, source_target_pairs={{0,2},{1,3},{2,0},{3,1},{4,6},{5,7},{6,4},{7,5},{8,10},{9,11},{10,... | collective-permute-start | bytes 737288 | tf_op jit(solution)/shard_map/ppermute | solution.py:436
  259.5 43.1 %collective-permute-start.61 = (bf16[1568,768]{1,0:T(8,128)(2,1)S(1)}, bf16[1568,768]{1,0:T(8,128)(2,1)S(1)}, u32[]{:S(2)}, u32[]{:S(2)}) collective-permute-start(bf16[1568,768]{1,0:T(8,128)(2,1)S(1)} %attn_dw0.1.refs_0_), channel_id=1, source_target_pairs={{16,0},{17,1},{18,2},{19,3},{20,4},{21,5},{22,6},{23,7},{24,8},{25... | collective-permute-start | bytes 7225352 | tf_op jit(solution)/shard_map/ppermute | solution.py:462
  260.8 40.8 %collective-permute-start.62 = (bf16[1536,768]{1,0:T(8,128)(2,1)S(1)}, bf16[1536,768]{1,0:T(8,128)(2,1)S(1)}, u32[]{:S(2)}, u32[]{:S(2)}) collective-permute-start(bf16[1536,768]{1,0:T(8,128)(2,1)S(1)} %get-tuple-element.371), channel_id=1, source_target_pairs={{0,4},{4,0},{8,12},{12,8},{1,5},{5,1},{9,13},{13,9},{2,6},{6,2},{1... | collective-permute-start | bytes 7077896 | tf_op jit(solution)/shard_map/ppermute | solution.py:467
  303.6 31.8 %collective-permute-start.63 = (bf16[800,768]{1,0:T(8,128)(2,1)S(1)}, bf16[800,768]{1,0:T(8,128)(2,1)S(1)}, u32[]{:S(2)}, u32[]{:S(2)}) collective-permute-start(bf16[800,768]{1,0:T(8,128)(2,1)S(1)} %get-tuple-element.373), channel_id=1, source_target_pairs={{0,4},{4,0},{8,12},{12,8},{1,5},{5,1},{9,13},{13,9},{2,6},{6,2},{1... | collective-permute-start | bytes 3686408 | tf_op jit(solution)/shard_map/ppermute | solution.py:467
  305.6 34.6 %collective-permute-start.67 = (bf16[768,768]{1,0:T(8,128)(2,1)S(1)}, bf16[768,768]{1,0:T(8,128)(2,1)S(1)}, u32[]{:S(2)}, u32[]{:S(2)}) collective-permute-start(bf16[768,768]{1,0:T(8,128)(2,1)S(1)} %get-tuple-element.393), channel_id=1, source_target_pairs={{16,24},{20,28},{24,16},{28,20},{17,25},{21,29},{25,17},{29,21},{1... | collective-permute-start | bytes 3538952 | tf_op jit(solution)/shard_map/ppermute | solution.py:467
  306.4 47.6 %collective-permute-start.66 = (bf16[768,768]{1,0:T(8,128)(2,1)S(1)}, bf16[768,768]{1,0:T(8,128)(2,1)S(1)}, u32[]{:S(2)}, u32[]{:S(2)}) collective-permute-start(bf16[768,768]{1,0:T(8,128)(2,1)S(1)} %get-tuple-element.391), channel_id=1, source_target_pairs={{0,8},{4,12},{8,0},{12,4},{1,9},{5,13},{9,1},{13,5},{2,10},{6,14},... | collective-permute-start | bytes 3538952 | tf_op jit(solution)/shard_map/ppermute | solution.py:467
  310.9 31.3 %collective-permute-start.65 = (bf16[416,768]{1,0:T(8,128)(2,1)S(1)}, bf16[416,768]{1,0:T(8,128)(2,1)S(1)}, u32[]{:S(2)}, u32[]{:S(2)}) collective-permute-start(bf16[416,768]{1,0:T(8,128)(2,1)S(1)} %get-tuple-element.377), channel_id=1, source_target_pairs={{16,24},{20,28},{24,16},{28,20},{17,25},{21,29},{25,17},{29,21},{1... | collective-permute-start | bytes 1916936 | tf_op jit(solution)/shard_map/ppermute | solution.py:467
  336.2 24.7 %collective-permute-start.64 = (bf16[416,768]{1,0:T(8,128)(2,1)S(1)}, bf16[416,768]{1,0:T(8,128)(2,1)S(1)}, u32[]{:S(2)}, u32[]{:S(2)}) collective-permute-start(bf16[416,768]{1,0:T(8,128)(2,1)S(1)} %get-tuple-element.375), channel_id=1, source_target_pairs={{0,8},{4,12},{8,0},{12,4},{1,9},{5,13},{9,1},{13,5},{2,10},{6,14},... | collective-permute-start | bytes 1916936 | tf_op jit(solution)/shard_map/ppermute | solution.py:467
  (48 other events, 366.5 us)
